TPU v7x, 32 devices: a whole 2x2x4 slice. The times are simulated.
32 devices in a mesh: seq: 16 (over z, x, core), head: 2 (over y).
Axes of the slice: x: 2, y: 2, z: 4, core: 2. Of those that a mesh axis runs over, the one named last changes fastest.
Arguments:
- alignment_rows: bfloat16 [128, 1024, 256], P('seq'), may hold values from -16 to 16
- upstream_derivative_tensor: bfloat16 [128, 1024, 256], P(None, 'seq'), may hold values from -12 to 12
- saved_pair_bias: bfloat16 [8, 1024, 1024], P('head', 'seq'), may hold values from -360 to 360
- pairwise_features: bfloat16 [1024, 1024, 128], P('seq', 'head'), may hold values from -16 to 16
- sequence_layernorm_scaling: float32 [256], replicated, may hold values from 0.5 to 2
- sequence_layernorm_centre: float32 [256], replicated, may hold values from -1 to 1
- asking_projection_matrix: bfloat16 [256, 256], replicated, may hold values from -0.375 to 0.375
- matching_projection_matrix: bfloat16 [256, 256], replicated, may hold values from -0.375 to 0.375
- content_projection_matrix: bfloat16 [256, 256], replicated, may hold values from -0.375 to 0.375
- sigmoid_projection_matrix: bfloat16 [256, 256], replicated, may hold values from -0.375 to 0.375
- gate_offset_bias: float32 [256], replicated, may hold values from -2 to 2
- final_projection_matrix: bfloat16 [256, 256], replicated, may hold values from -0.375 to 0.375
- pairwise_norm_gain: float32 [128], replicated, may hold values from 0.5 to 2
- pairwise_weight: bfloat16 [128, 8], replicated, may hold values from -0.5 to 0.5
Outputs:
- alignment_input_gradient: bfloat16 [128, 1024, 256], P('seq', 'head')
- pairwise_gradient: bfloat16 [1024, 1024, 128], P('seq', 'head')
All inputs are finite; a program needn't handle non-finite values.
Results may differ from a plain program's by a relative error of at most 0.012.
The roundings to bfloat16 on the way count: a program that leaves them out, or rounds other values in their place, can miss the bound.
Values may be sent and summed in bfloat16 or wider, within the bound.
A program may use at most 320 MiB of HBM per device.

v0:
```python
import jax
import jax.numpy as jnp
from jax import lax
from jax.experimental import pallas as pl
from jax.experimental.pallas import tpu as pltpu
from jax.sharding import PartitionSpec as P

SUBSPACE_WIDTH = 32


epsilon = 1e-05


def layer_statistics(values):
    average = jnp.mean(values, axis=-1, keepdims=True)
    centred = values - average
    inverse_deviation = lax.rsqrt(jnp.mean(centred * centred, axis=-1, keepdims=True) + epsilon)
    return (centred * inverse_deviation, inverse_deviation)


def layer_reverse_step(upstream, standardized_values, inverse_deviation):
    first_mean = jnp.mean(upstream, axis=-1, keepdims=True)
    second_mean = jnp.mean(upstream * standardized_values, axis=-1, keepdims=True)
    return inverse_deviation * (upstream - first_mean - standardized_values * second_mean)


def dot(left, right, left_dim, right_dim):
    return lax.dot_general(
        left, right, (((left_dim,), (right_dim,)), ((), ())), preferred_element_type=jnp.float32
    )


def attention_kernel(tile, q_ref, k_ref, v_ref, gate_ref, gd_ref, bias_ref, grads_ref, sum_ref, acc_ref):
    score_scale = SUBSPACE_WIDTH ** (-0.5)
    residues = acc_ref.shape[0]

    @pl.when(pl.program_id(0) == 0)
    def _():
        acc_ref[...] = jnp.zeros_like(acc_ref)

    keys_t = k_ref[...]
    vals_t = v_ref[...]
    key_grad = jnp.zeros((SUBSPACE_WIDTH, residues), jnp.float32)
    value_grad = jnp.zeros((SUBSPACE_WIDTH, residues), jnp.float32)
    for start in range(0, residues, tile):
        rows = slice(start, start + tile)
        query_t = q_ref[:, rows]
        query = query_t.astype(jnp.float32).T.astype(jnp.bfloat16)
        logits = dot(query, keys_t, 1, 0) + bias_ref[rows, :].astype(jnp.float32)
        top = jnp.max(logits, axis=-1, keepdims=True)
        weights = jnp.exp(logits - top)
        share = 1.0 / jnp.sum(weights, axis=-1, keepdims=True)
        weights_low = weights.astype(jnp.bfloat16)
        attended = dot(weights_low, vals_t, 1, 1) * share
        gate_t = gate_ref[:, rows]
        grad_t = gd_ref[:, rows].astype(jnp.float32)
        out_grad = (grad_t * gate_t).astype(jnp.bfloat16).astype(jnp.float32).T
        scaled = out_grad * share
        inner = jnp.sum(scaled * attended, axis=-1, keepdims=True)
        prob_grad = dot(scaled.astype(jnp.bfloat16), vals_t, 1, 0)
        score_grad = weights * (prob_grad - inner)
        acc_ref[rows, :] += score_grad
        score_low = score_grad.astype(jnp.bfloat16)
        query_grad = score_scale * dot(score_low, keys_t, 1, 1)
        key_grad += dot(query_t, score_low, 1, 0)
        value_grad += dot(scaled.T.astype(jnp.bfloat16), weights_low, 1, 0)
        gate_grad = grad_t * attended.T * gate_t * (1.0 - gate_t)
        grads_ref[0, :, rows] = query_grad.T.astype(jnp.bfloat16)
        grads_ref[3, :, rows] = gate_grad.astype(jnp.bfloat16)
    grads_ref[1] = key_grad.astype(jnp.bfloat16)
    grads_ref[2] = value_grad.astype(jnp.bfloat16)

    @pl.when(pl.program_id(0) == pl.num_programs(0) - 1)
    def _():
        sum_ref[...] = acc_ref[...].astype(jnp.bfloat16)


def attention_reverse(head, projected, gate, gated_grad, bias_head):
    rows, _, _, width, residues = projected.shape
    tile = 256

    def part(which):
        return pl.BlockSpec(
            (None, None, None, width, residues), lambda s: (s, which, head, 0, 0)
        )

    plain = pl.BlockSpec((None, None, width, residues), lambda s: (s, head, 0, 0))
    square = rows * residues * residues
    return pl.pallas_call(
        lambda *refs: attention_kernel(tile, *refs),
        grid=(rows,),
        in_specs=[
            part(0),
            part(1),
            part(2),
            plain,
            plain,
            pl.BlockSpec((residues, residues), lambda s: (0, 0)),
        ],
        out_specs=[
            pl.BlockSpec((None, 4, width, residues), lambda s: (s, 0, 0, 0)),
            pl.BlockSpec((residues, residues), lambda s: (0, 0)),
        ],
        out_shape=[
            jax.ShapeDtypeStruct((rows, 4, width, residues), jnp.bfloat16),
            jax.ShapeDtypeStruct((residues, residues), jnp.bfloat16),
        ],
        scratch_shapes=[pltpu.VMEM((residues, residues), jnp.float32)],
        cost_estimate=pl.CostEstimate(
            flops=100 * 2 * width * square // 8, bytes_accessed=12 << 20, transcendentals=square
        ),
        compiler_params=pltpu.CompilerParams(vmem_limit_bytes=40 << 20),
        name="attention_reverse_%d" % head,
    )(projected, projected, projected, gate, gated_grad, bias_head)


def per_device(
    alignment_rows,
    upstream_derivative_tensor,
    saved_pair_bias,
    pairwise_features,
    sequence_layernorm_scaling,
    sequence_layernorm_centre,
    asking_projection_matrix,
    matching_projection_matrix,
    content_projection_matrix,
    sigmoid_projection_matrix,
    gate_offset_bias,
    final_projection_matrix,
    pairwise_norm_gain,
    pairwise_weight,
):
    local_heads = saved_pair_bias.shape[0]
    all_heads = pairwise_weight.shape[1]
    resident_rows, residue_total, channel_count = alignment_rows.shape
    head_width = local_heads * SUBSPACE_WIDTH
    first_head = lax.axis_index("head") * local_heads
    first_col = first_head * SUBSPACE_WIDTH
    score_scale = SUBSPACE_WIDTH ** (-0.5)
    biases = [
        lax.all_gather(saved_pair_bias[head], "seq", axis=0, tiled=True)
        for head in range(local_heads)
    ]
    row_grads = lax.all_to_all(
        upstream_derivative_tensor, "seq", split_axis=0, concat_axis=1, tiled=True
    )
    standardized_values, inverse_deviation = layer_statistics(alignment_rows.astype(jnp.float32))
    normalized_rows = (
        standardized_values * sequence_layernorm_scaling + sequence_layernorm_centre
    ).astype(jnp.bfloat16)

    def local(coefficient_matrix):
        return lax.dynamic_slice_in_dim(coefficient_matrix, first_col, head_width, 1)

    stacked = jnp.concatenate(
        [
            local(asking_projection_matrix),
            local(matching_projection_matrix),
            local(content_projection_matrix),
            local(sigmoid_projection_matrix),
        ],
        axis=1,
    )
    raw = jnp.einsum("cf,src->sfr", stacked, normalized_rows, preferred_element_type=jnp.float32)
    factor = jnp.where(jnp.arange(3 * head_width) < head_width, score_scale, 1.0)
    projected = (
        (raw[:, : 3 * head_width] * factor[:, None])
        .astype(jnp.bfloat16)
        .reshape(resident_rows, 3, local_heads, SUBSPACE_WIDTH, residue_total)
    )
    gate_shift = lax.dynamic_slice_in_dim(gate_offset_bias, first_col, head_width, 0)
    channel_shape = (resident_rows, local_heads, SUBSPACE_WIDTH, residue_total)
    gate = jax.nn.sigmoid(raw[:, 3 * head_width :] + gate_shift[:, None]).reshape(channel_shape)
    out_rows = lax.dynamic_slice_in_dim(final_projection_matrix, first_col, head_width, 0)
    gated_grad = (
        jnp.einsum("wc,src->swr", out_rows, row_grads, preferred_element_type=jnp.float32)
        .astype(jnp.bfloat16)
        .reshape(channel_shape)
    )
    head_grads = []
    summed_heads = []
    for head in range(local_heads):
        grads, bias_grad = attention_reverse(head, projected, gate, gated_grad, biases[head])
        head_grads.append(grads)
        summed_heads.append(lax.psum_scatter(bias_grad, "seq", scatter_dimension=0, tiled=True))
    summed_rows = jnp.stack(summed_heads)
    head_grad_rows = jnp.stack(head_grads, axis=1).reshape(
        resident_rows, local_heads, 4 * SUBSPACE_WIDTH, residue_total
    )
    piled_arrays = jnp.stack(
        [
            coefficient_matrix.reshape(channel_count, all_heads, SUBSPACE_WIDTH)
            for coefficient_matrix in (
                asking_projection_matrix,
                matching_projection_matrix,
                content_projection_matrix,
                sigmoid_projection_matrix,
            )
        ],
        axis=2,
    )
    piled_arrays = piled_arrays.reshape(channel_count, all_heads, 4 * SUBSPACE_WIDTH)
    local_weight = lax.dynamic_slice_in_dim(piled_arrays, first_head, local_heads, 1)
    partial_term = jnp.einsum(
        "shfr,chf->src", head_grad_rows, local_weight, preferred_element_type=jnp.float32
    )
    normalized_gradient = lax.psum_scatter(
        partial_term.astype(jnp.bfloat16), "head", scatter_dimension=1, tiled=True
    ).astype(jnp.float32)
    block_len = residue_total // lax.axis_size("head")
    block_start = lax.axis_index("head") * block_len
    normalized_block = lax.dynamic_slice_in_dim(standardized_values, block_start, block_len, 1)
    inverse_spread_block = lax.dynamic_slice_in_dim(inverse_deviation, block_start, block_len, 1)
    alignment_input_gradient = layer_reverse_step(
        normalized_gradient * sequence_layernorm_scaling, normalized_block, inverse_spread_block
    ).astype(jnp.bfloat16)
    bias_tile = lax.all_to_all(
        summed_rows.astype(jnp.bfloat16), "head", split_axis=2, concat_axis=0, tiled=True
    ).astype(summed_rows.dtype)
    bias_low = bias_tile.astype(jnp.bfloat16)
    pair_hat, pair_inv = layer_statistics(pairwise_features.astype(jnp.float32))
    pair_normed_grad = jnp.einsum(
        "hij,ch->ijc", bias_low, pairwise_weight, preferred_element_type=jnp.float32
    )
    pairwise_gradient = layer_reverse_step(
        pair_normed_grad * pairwise_norm_gain, pair_hat, pair_inv
    ).astype(jnp.bfloat16)
    return (alignment_input_gradient, pairwise_gradient)


def solution(mesh):
    placed = (
        P("seq", None, None),
        P(None, "seq", None),
        P("head", "seq", None),
        P("seq", "head", None),
        P(),
        P(),
        P(),
        P(),
        P(),
        P(),
        P(),
        P(),
        P(),
        P(),
    )
    return jax.shard_map(
        per_device,
        mesh=mesh,
        in_specs=placed,
        out_specs=(P("seq", "head", None), P("seq", "head", None)),
        check_vma=False,
    )
```

profile of v0, /device:TPU:0, one launch (start us, length us, event | category | flops | bytes accessed | tf_op | source)
XLA Modules:
  0.0 567.5 jit_solution(14991655232751190059)
XLA Ops:
  7.3 2.0 fusion.48
  10.1 7.4 %all-to-all-start = ((bf16[128,64,256]{2,1,0:T(8,128)(2,1)}), bf16[128,64,256]{2,1,0:T(8,128)(2,1)}, u32[]{:S(2)}, u32[]{:S(2)}) async-start(bf16[128,64,256]{2,1,0:T(8,128)(2,1)} %param.15), calls=%async_computation | async-start | bytes 8388608 | tf_op jit(solution)/shard_map/all_to_all | solution.py:144
  19.5 3.6 convert_reduce_fusion.1
  23.2 4.0 fusion.12
  27.2 2.5 convolution_bitcast_fusion
  29.8 5.7 %copy-done.19 = f32[8,512,1024]{2,1,0:T(8,128)} copy-done((f32[8,512,1024]{2,1,0:T(8,128)}, f32[8,512,1024]{2,1,0:T(8,128)S(1)}, u32[]{:S(2)}) %copy-start.19) | copy-done | bytes 16777240
  35.5 3.1 fusion.24
  38.6 9.3 %fusion.9 = bf16[8,384,1024]{2,1,0:T(8,128)(2,1)} fusion(f32[8,512,1024]{2,1,0:T(8,128)} %copy-done.19, f32[384]{0:T(512)S(1)} %fusion.45), kind=kLoop, calls=%fused_computation.13 | loop fusion | flops 6291456 | bytes 18875904 | tf_op jit(solution)/shard_map/convert_element_type | solution.py:168
  48.0 59.7 %all-to-all-done = bf16[128,64,256]{2,1,0:T(8,128)(2,1)} async-done(((bf16[128,64,256]{2,1,0:T(8,128)(2,1)}), bf16[128,64,256]{2,1,0:T(8,128)(2,1)}, u32[]{:S(2)}, u32[]{:S(2)}) %all-to-all-start) | async-done | bytes 4194336 | tf_op jit(solution)/shard_map/all_to_all | solution.py:144
  107.7 2.5 copy.54
  110.2 1.5 convolution_convert_fusion
  111.8 2.3 copy-done.2
  114.0 1.6 copy-done.18
  115.6 39.0 %attention_reverse_3.1 = (bf16[8,4,32,1024]{3,2,1,0:T(8,128)(2,1)S(1)}, bf16[1024,1024]{1,0:T(8,128)(2,1)S(1)}) custom-call(bf16[8,3,4,32,1024]{4,3,2,1,0:T(8,128)(2,1)} %bitcast.70, bf16[8,3,4,32,1024]{4,3,2,1,0:T(8,128)(2,1)} %bitcast.71, bf16[8,3,4,32,1024]{4,3,2,1,0:T(8,128)(2,1)} %bitcast.72, f32[8,4,32,1024]{3,2,1,0:T(8,128)S(1)} %bitcast.54, ...), custom_call_target="tpu_custom_call" | custom-call | flops 6710886400 | bytes 12582912 | tf_op jit(solution)/shard_map/attention_reverse_3/pallas_call | solution.py:89
  154.6 1.4 copy-done.6
  157.4 2.2 copy-done.3
  159.6 1.6 copy-done.17
  161.2 38.8 %attention_reverse_2.1 = (bf16[8,4,32,1024]{3,2,1,0:T(8,128)(2,1)S(1)}, bf16[1024,1024]{1,0:T(8,128)(2,1)S(1)}) custom-call(bf16[8,3,4,32,1024]{4,3,2,1,0:T(8,128)(2,1)} %bitcast.73, bf16[8,3,4,32,1024]{4,3,2,1,0:T(8,128)(2,1)} %bitcast.74, bf16[8,3,4,32,1024]{4,3,2,1,0:T(8,128)(2,1)} %bitcast.75, f32[8,4,32,1024]{3,2,1,0:T(8,128)S(1)} %bitcast.55, ...), custom_call_target="tpu_custom_call" | custom-call | flops 6710886400 | bytes 12582912 | tf_op jit(solution)/shard_map/attention_reverse_2/pallas_call | solution.py:89
  201.4 1.4 copy-done.11
  202.9 2.2 copy-done.4
  205.1 1.6 copy-done.16
  206.6 39.0 %attention_reverse_1.1 = (bf16[8,4,32,1024]{3,2,1,0:T(8,128)(2,1)S(1)}, bf16[1024,1024]{1,0:T(8,128)(2,1)S(1)}) custom-call(bf16[8,3,4,32,1024]{4,3,2,1,0:T(8,128)(2,1)} %bitcast.76, bf16[8,3,4,32,1024]{4,3,2,1,0:T(8,128)(2,1)} %bitcast.77, bf16[8,3,4,32,1024]{4,3,2,1,0:T(8,128)(2,1)} %bitcast.78, f32[8,4,32,1024]{3,2,1,0:T(8,128)S(1)} %bitcast.56, ...), custom_call_target="tpu_custom_call" | custom-call | flops 6710886400 | bytes 12582912 | tf_op jit(solution)/shard_map/attention_reverse_1/pallas_call | solution.py:89
  247.0 1.4 copy-done.13
  248.5 2.3 copy-done.5
  250.8 1.7 copy-done.15
  252.4 38.8 %attention_reverse_0.1 = (bf16[8,4,32,1024]{3,2,1,0:T(8,128)(2,1)S(1)}, bf16[1024,1024]{1,0:T(8,128)(2,1)S(1)}) custom-call(bf16[8,3,4,32,1024]{4,3,2,1,0:T(8,128)(2,1)} %bitcast.79, bf16[8,3,4,32,1024]{4,3,2,1,0:T(8,128)(2,1)} %bitcast.80, bf16[8,3,4,32,1024]{4,3,2,1,0:T(8,128)(2,1)} %bitcast.81, f32[8,4,32,1024]{3,2,1,0:T(8,128)S(1)} %bitcast.57, ...), custom_call_target="tpu_custom_call" | custom-call | flops 6710886400 | bytes 12582912 | tf_op jit(solution)/shard_map/attention_reverse_0/pallas_call | solution.py:89
  292.6 1.4 copy-done.14
  294.1 4.4 copy.58
  298.5 2.4 copy.57
  300.8 4.1 copy.56
  304.9 4.0 copy.55
  308.9 5.9 %bitcast_convert_fusion = bf16[8,1024,256]{2,1,0:T(8,128)(2,1)} fusion(bf16[8,1,128,1024]{2,3,1,0:T(8,128)(2,1)S(1)} %copy-done.22, bf16[8,1,128,1024]{2,3,1,0:T(8,128)(2,1)} %copy.57, bf16[8,1,128,1024]{2,3,1,0:T(8,128)(2,1)} %copy.56, bf16[8,1,128,1024]{2,3,1,0:T(8,128)(2,1)} %copy.55, bf16[256,8,128]{0,2,1:T(8,128)(2,1)S(1)} %bitcast.92, s32[]{:T(128)S(6)} %select_n.26), kind=kOutput, calls=%fused_computation.28 | convolution fusion | flops 2162163712 | bytes 12845060 | tf_op jit(solution)/shard_map/shfr,chf->src/dot_general | solution.py:204
  314.8 12.0 %copy.65 = bf16[64,512,128]{1,2,0:T(8,128)(2,1)} copy(bf16[64,512,128]{2,1,0:T(8,128)(2,1)} %param.17) | data formatting | bytes 16777216 | tf_op args[3]
  326.7 5.9 %convert_reduce_fusion = f32[64,512]{1,0:T(8,128)S(1)} fusion(bf16[64,512,128]{1,2,0:T(8,128)(2,1)} %copy.65), kind=kLoop, calls=%fused_computation.1 | loop fusion | flops 8355840 | bytes 8519680 | tf_op jit(solution)/shard_map/reduce_sum | solution.py:15
  332.7 5.2 fusion.10
  337.9 3.1 fusion.8
  341.1 21.1 %reduce-scatter.12.cloned.1.call-done = bf16[64,1024]{1,0:T(8,128)(2,1)} async-done(((bf16[1024,1024]{1,0:T(8,128)(2,1)}), bf16[64,1024]{1,0:T(8,128)(2,1)}) %reduce-scatter.12.cloned.1.call-update) | async-done | bytes 131088 | tf_op jit(solution)/shard_map/reduce_scatter | solution.py:185
  362.2 64.5 %reduce-scatter.10.cloned.1.call-done = bf16[64,1024]{1,0:T(8,128)(2,1)} async-done(((bf16[1024,1024]{1,0:T(8,128)(2,1)}), bf16[64,1024]{1,0:T(8,128)(2,1)}) %reduce-scatter.10.cloned.1.call-update) | async-done | bytes 131088 | tf_op jit(solution)/shard_map/reduce_scatter | solution.py:185
  426.7 64.5 %reduce-scatter.8.cloned.1.call-done = bf16[64,1024]{1,0:T(8,128)(2,1)} async-done(((bf16[1024,1024]{1,0:T(8,128)(2,1)}), bf16[64,1024]{1,0:T(8,128)(2,1)}) %reduce-scatter.8.cloned.1.call-update) | async-done | bytes 131088 | tf_op jit(solution)/shard_map/reduce_scatter | solution.py:185
  493.1 1.5 reshape.102
  494.7 3.5 all-to-all-start.1
  498.2 12.9 %all-to-all-done.1 = bf16[2,2,65536]{2,1,0:T(2,128)(2,1)S(1)} async-done(((bf16[2,2,65536]{2,1,0:T(2,128)(2,1)}), bf16[2,2,65536]{2,1,0:T(2,128)(2,1)S(1)}, u32[]{:S(2)}, u32[]{:S(2)}) %all-to-all-start.1) | async-done | bytes 524320 | tf_op jit(solution)/shard_map/all_to_all | solution.py:217
  513.0 7.7 %multiply_reduce_fusion = (f32[64,512]{1,0:T(8,128)S(1)}, f32[64,512]{1,0:T(8,128)S(1)}, f32[64,512,128]{1,2,0:T(8,128)S(1)}) fusion(f32[128]{0:T(128)S(1)} %copy-done.29, f32[64,512]{1,0:T(8,128)S(1)} %add_rsqrt_fusion, f32[64,512]{1,0:T(8,128)S(1)} %broadcast_multiply_fusion.2, bf16[64,512,128]{1,2,0:T(8,128)(2,1)} %copy.65, ...), kind=kOutput, calls=%fused_computation.11 | convolution fusion | flops 96403456 | bytes 26216960 | tf_op jit(solution)/shard_map/hij,ch->ijc/dot_general | solution.py:222
  520.8 9.5 %fusion.7 = bf16[64,512,128]{1,2,0:T(8,128)(2,1)} fusion(bf16[64,512,128]{1,2,0:T(8,128)(2,1)} %copy.65, f32[64,512,128]{1,2,0:T(8,128)S(1)} %get-tuple-element.32, f32[64,512]{1,0:T(8,128)S(1)} %broadcast_multiply_fusion, f32[64,512]{1,0:T(8,128)S(1)} %broadcast_multiply_fusion.1, f32[128]{0:T(128)S(1)} %copy-done.29, f32[64,512]{1,0:T(8,128)S(1)} %add_rsqrt_fusion, ...), kind=kLoop, calls=%fused_computation.9 | loop fusion | flops 37748736 | bytes 34079232 | tf_op jit(solution)/shard_map/convert_element_type | solution.py:227
  530.3 11.9 %copy.68 = bf16[64,512,128]{2,1,0:T(8,128)(2,1)} copy(bf16[64,512,128]{1,2,0:T(8,128)(2,1)} %fusion.7) | data formatting | bytes 16777216
  542.2 8.7 %reduce-scatter.6.cloned.1.call-done = bf16[8,512,256]{2,1,0:T(8,128)(2,1)} async-done(((bf16[8,1024,256]{2,1,0:T(8,128)(2,1)}), bf16[8,512,256]{2,1,0:T(8,128)(2,1)}) %reduce-scatter.6.cloned.1.call-update) | async-done | bytes 2097168 | tf_op jit(solution)/shard_map/reduce_scatter | solution.py:207
  551.0 4.0 fusion.25
  555.0 5.5 multiply_convert_fusion
  (103 shorter events, 12.3 us)
Async XLA Ops:
  7.2 103.1 %copy-start = (bf16[256,256]{1,0:T(8,128)(2,1)S(1)}, bf16[256,256]{1,0:T(8,128)(2,1)}, u32[]{:S(2)}) copy-start(bf16[256,256]{1,0:T(8,128)(2,1)} %param.25) | copy-start | bytes 393220
  7.2 11.8 %copy-start.23 = (bf16[256,256]{1,0:T(8,128)(2,1)S(1)}, bf16[256,256]{1,0:T(8,128)(2,1)}, u32[]{:S(2)}) copy-start(bf16[256,256]{1,0:T(8,128)(2,1)} %param.23) | copy-start | bytes 393220
  7.2 11.9 %copy-start.24 = (bf16[256,256]{1,0:T(8,128)(2,1)S(1)}, bf16[256,256]{1,0:T(8,128)(2,1)}, u32[]{:S(2)}) copy-start(bf16[256,256]{1,0:T(8,128)(2,1)} %param.22) | copy-start | bytes 393220
  7.2 12.0 %copy-start.25 = (bf16[256,256]{1,0:T(8,128)(2,1)S(1)}, bf16[256,256]{1,0:T(8,128)(2,1)}, u32[]{:S(2)}) copy-start(bf16[256,256]{1,0:T(8,128)(2,1)} %param.21) | copy-start | bytes 393220
  7.2 12.1 %copy-start.26 = (bf16[256,256]{1,0:T(8,128)(2,1)S(1)}, bf16[256,256]{1,0:T(8,128)(2,1)}, u32[]{:S(2)}) copy-start(bf16[256,256]{1,0:T(8,128)(2,1)} %param.20) | copy-start | bytes 393220
  7.2 12.2 %copy-start.31 = (f32[256]{0:T(256)S(1)}, f32[256]{0:T(256)}, u32[]{:S(2)}) copy-start(f32[256]{0:T(256)} %param.24) | copy-start | bytes 3076
  7.2 104.5 %all-gather.15.cloned.1.call-start = ((), (), s32[]{:S(2)}) async-start(), calls=%async_computation.15 | async-start | bytes 2228224 | tf_op jit(solution)/shard_map/all_gather | solution.py:141
  9.3 148.0 %all-gather.13.cloned.1.call-start = ((), (), s32[]{:S(2)}) async-start(), calls=%async_computation.14 | async-start | bytes 2228224 | tf_op jit(solution)/shard_map/all_gather | solution.py:141
  10.1 17.1 %copy-start.27 = (f32[256]{0:T(256)S(1)}, f32[256]{0:T(256)}, u32[]{:S(2)}) copy-start(f32[256]{0:T(256)} %param.18) | copy-start | bytes 3076
  10.1 17.1 %copy-start.28 = (f32[256]{0:T(256)S(1)}, f32[256]{0:T(256)}, u32[]{:S(2)}) copy-start(f32[256]{0:T(256)} %param.19) | copy-start | bytes 3076
  10.1 97.6 %all-to-all-start = ((bf16[128,64,256]{2,1,0:T(8,128)(2,1)}), bf16[128,64,256]{2,1,0:T(8,128)(2,1)}, u32[]{:S(2)}, u32[]{:S(2)}) async-start(bf16[128,64,256]{2,1,0:T(8,128)(2,1)} %param.15), calls=%async_computation | async-start | bytes 8388608 | tf_op jit(solution)/shard_map/all_to_all | solution.py:144
  17.6 185.3 %all-gather.11.cloned.1.call-start = ((), (), s32[]{:S(2)}) async-start(), calls=%async_computation.13 | async-start | bytes 2228224 | tf_op jit(solution)/shard_map/all_gather | solution.py:141
  18.3 230.1 %all-gather.9.cloned.1.call-start = ((), (), s32[]{:S(2)}) async-start(), calls=%async_computation.12 | async-start | bytes 2228224 | tf_op jit(solution)/shard_map/all_gather | solution.py:141
  18.9 322.2 %reduce-scatter.14.cloned.1.call-start = ((), (), s32[]{:S(2)}) async-start(), calls=%async_computation.11 | async-start | bytes 2228224 | tf_op jit(solution)/shard_map/reduce_scatter | solution.py:185
  19.4 7.8 %copy-start.20 = (bf16[8,1024,256]{2,1,0:T(8,128)(2,1)S(1)}, bf16[8,1024,256]{2,1,0:T(8,128)(2,1)}, u32[]{:S(2)}) copy-start(bf16[8,1024,256]{2,1,0:T(8,128)(2,1)} %param.14) | copy-start | bytes 12582916
  29.8 5.8 %copy-start.19 = (f32[8,512,1024]{2,1,0:T(8,128)}, f32[8,512,1024]{2,1,0:T(8,128)S(1)}, u32[]{:S(2)}) copy-start(f32[8,512,1024]{2,1,0:T(8,128)S(1)} %convolution_bitcast_fusion) | copy-start | bytes 50331652
  111.7 2.3 copy-start.2
  114.0 1.6 copy-start.18
  154.6 1.4 copy-start.6
  156.0 1.3 copy-start.9
  157.3 204.9 %reduce-scatter.12.cloned.1.call-start = ((), (), s32[]{:S(2)}) async-start(), calls=%async_computation.10 | async-start | bytes 2228224 | tf_op jit(solution)/shard_map/reduce_scatter | solution.py:185
  157.4 2.2 copy-start.3
  159.6 1.6 copy-start.17
  200.0 1.4 copy-start.7
  201.4 1.4 copy-start.11
  202.8 223.9 %reduce-scatter.10.cloned.1.call-start = ((), (), s32[]{:S(2)}) async-start(), calls=%async_computation.9 | async-start | bytes 2228224 | tf_op jit(solution)/shard_map/reduce_scatter | solution.py:185
  202.9 2.2 copy-start.4
  205.0 1.6 copy-start.16
  245.7 1.3 copy-start.8
  247.0 1.4 copy-start.13
  248.4 242.8 %reduce-scatter.8.cloned.1.call-start = ((), (), s32[]{:S(2)}) async-start(), calls=%async_computation.8 | async-start | bytes 2228224 | tf_op jit(solution)/shard_map/reduce_scatter | solution.py:185
  248.5 2.3 copy-start.5
  250.8 1.7 copy-start.15
  291.3 1.3 copy-start.10
  292.6 1.4 copy-start.14
  293.9 4.6 copy-start.12
  293.9 257.1 %reduce-scatter.6.cloned.1.call-start = ((), (), s32[]{:S(2)}) async-start(), calls=%async_computation.7 | async-start | bytes 6291456 | tf_op jit(solution)/shard_map/reduce_scatter | solution.py:207
  300.8 8.1 %copy-start.22 = (bf16[8,1,128,1024]{2,3,1,0:T(8,128)(2,1)S(1)}, bf16[8,1,128,1024]{2,3,1,0:T(8,128)(2,1)}, u32[]{:S(2)}) copy-start(bf16[8,1,128,1024]{2,3,1,0:T(8,128)(2,1)} %copy.58) | copy-start | bytes 6291460
  326.7 5.9 %copy-start.21 = (bf16[8,1024,256]{2,1,0:T(8,128)(2,1)S(1)}, bf16[8,1024,256]{2,1,0:T(8,128)(2,1)}, u32[]{:S(2)}) copy-start(bf16[8,1024,256]{2,1,0:T(8,128)(2,1)} %param.14) | copy-start | bytes 12582916
  326.7 11.2 %slice-start = ((s8[8388608]{0:T(1024)(128)(4,1)}), s8[4194304]{0:T(1024)(128)(4,1)S(1)}, s32[]{:S(2)}) async-start(s8[8388608]{0:T(1024)(128)(4,1)} %bitcast.82), calls=%async_computation.16 | async-start | bytes 8388608
  332.6 5.2 slice-start.1
  337.9 175.1 %copy-start.29 = (f32[128]{0:T(128)S(1)}, f32[128]{0:T(128)}, u32[]{:S(2)}) copy-start(f32[128]{0:T(128)} %param.26) | copy-start | bytes 1540
  337.9 175.1 %copy-start.30 = (bf16[128,8]{0,1:T(8,128)(2,1)S(1)}, bf16[128,8]{0,1:T(8,128)(2,1)}, u32[]{:S(2)}) copy-start(bf16[128,8]{0,1:T(8,128)(2,1)} %param.27) | copy-start | bytes 6148
  494.7 16.4 %all-to-all-start.1 = ((bf16[2,2,65536]{2,1,0:T(2,128)(2,1)}), bf16[2,2,65536]{2,1,0:T(2,128)(2,1)S(1)}, u32[]{:S(2)}, u32[]{:S(2)}) async-start(bf16[2,2,65536]{2,1,0:T(2,128)(2,1)} %reshape.102), calls=%async_computation.6 | async-start | bytes 1048576 | tf_op jit(solution)/shard_map/all_to_all | solution.py:217
  530.3 30.2 %copy-start.1 = (bf16[256,256]{1,0:T(8,128)(2,1)S(1)}, bf16[256,256]{1,0:T(8,128)(2,1)}, u32[]{:S(2)}) copy-start(bf16[256,256]{1,0:T(8,128)(2,1)} %param.25) | copy-start | bytes 393220
Sparse Core Ops, SparseCore 0:
  10.8 86.4 all-gather.14
  99.4 49.5 all-gather.12
  151.2 40.2 all-gather.10
  193.5 40.1 all-gather.8
  237.3 60.5 reduce-scatter.13
  301.5 60.6 reduce-scatter.11
  365.9 60.7 reduce-scatter.9
  430.5 60.7 reduce-scatter.7
  493.5 57.4 reduce-scatter.5
where the time goes:
time: 576 us; the launch traced here: 568 us
  waiting for transfers between devices  234 us (41%)
  Pallas kernels  156 us (27%)
  local copies, waits for them, and re-layouts  79.9 us (14%)
  other arithmetic  54.6 us (9%)
  matrix products  17.6 us (3%)
  between operations  14.9 us (3%)
  starting transfers between devices  11.3 us (2%)
    pallas_call x4, Pallas kernels, attention_reverse(): pl.pallas_call(lambda *refs: attention_kernel(tile, *refs), grid=(rows,),...  156 us
    reduce_scatter x4, waiting for transfers between devices, per_device(): lax.psum_scatter(bias_grad, 'seq', scatter_dimension=0, tiled=True)  150 us
    all_to_all x1, waiting for transfers between devices, per_device(): lax.all_to_all(upstream_derivative_tensor, 'seq', split_axis=0, concat_ax...  59.7 us
    unnamed x76, local copies, waits for them, and re-layouts  58.9 us
    another operation x4, local copies, waits for them, and re-layouts, per_device(): jnp.stack(head_grads, axis=1)  14.8 us
    all_to_all x1, waiting for transfers between devices, per_device(): lax.all_to_all(summed_rows.astype(jnp.bfloat16), 'head', split_axis=2, co...  12.9 us
  transfers between devices with their start and end apart: 11, of which 6 were waited for; matrix products, arithmetic and copies ran while one was open for 19% of the time, Pallas kernels for 27%

commit v1 on v0

v1 whole, which is shorter than its diff:
```python
import jax
import jax.numpy as jnp
from jax import lax
from jax.experimental import pallas as pl
from jax.experimental.pallas import tpu as pltpu
from jax.sharding import PartitionSpec as P


SUBSPACE_WIDTH = 32
LANES = 128
PACK = LANES // SUBSPACE_WIDTH
VMEM_LIMIT = 60 << 20

epsilon = 1e-05


def dot(left, right, left_dim, right_dim):
    return lax.dot_general(
        left, right, (((left_dim,), (right_dim,)), ((), ())), preferred_element_type=jnp.float32
    )


def layer_statistics(values):
    average = jnp.mean(values, axis=-1, keepdims=True)
    centred = values - average
    inverse_deviation = lax.rsqrt(jnp.mean(centred * centred, axis=-1, keepdims=True) + epsilon)
    return (centred * inverse_deviation, inverse_deviation)


def layer_reverse_step(upstream, standardized_values, inverse_deviation):
    first_mean = jnp.mean(upstream, axis=-1, keepdims=True)
    second_mean = jnp.mean(upstream * standardized_values, axis=-1, keepdims=True)
    return inverse_deviation * (upstream - first_mean - standardized_values * second_mean)


def params():
    return pltpu.CompilerParams(vmem_limit_bytes=VMEM_LIMIT)


def upstream_kernel(heads, up_ref, w_ref, *out_refs):
    rows, residues, channels = up_ref.shape
    group = residues // PACK
    total = None
    for k in range(PACK):
        part = up_ref[:, k * group : (k + 1) * group, :].reshape(rows * group, channels)
        term = dot(part, w_ref[k], 1, 0)
        total = term if total is None else total + term
    for h in range(heads):
        out_refs[h][...] = (
            total[:, h * LANES : (h + 1) * LANES].astype(jnp.bfloat16).reshape(rows, group, LANES)
        )


def project_upstream(upstream, out_rows, heads):
    total_rows, residues, channels = upstream.shape
    weight = out_rows.reshape(heads, SUBSPACE_WIDTH, channels)
    select = jnp.eye(PACK, dtype=weight.dtype)
    padded = jnp.einsum("kp,hdc->kchpd", select, weight).reshape(PACK, channels, heads * LANES)
    block = 32
    group = residues // PACK
    return pl.pallas_call(
        lambda *refs: upstream_kernel(heads, *refs),
        grid=(total_rows // block,),
        in_specs=[
            pl.BlockSpec((block, residues, channels), lambda s: (s, 0, 0)),
            pl.BlockSpec((PACK, channels, heads * LANES), lambda s: (0, 0, 0)),
        ],
        out_specs=[pl.BlockSpec((block, group, LANES), lambda s: (s, 0, 0))] * heads,
        out_shape=[jax.ShapeDtypeStruct((total_rows, group, LANES), jnp.bfloat16)] * heads,
        cost_estimate=pl.CostEstimate(
            flops=2 * upstream.size * heads * LANES, bytes_accessed=8 << 20, transcendentals=0
        ),
        compiler_params=params(),
        name="upstream_projection",
    )(upstream, padded)


def rows_kernel(heads, x_ref, gain_ref, centre_ref, w_ref, wg_ref, shift_ref, out_ref, gate_ref):
    hat, _ = layer_statistics(x_ref[...].astype(jnp.float32))
    normed = (hat * gain_ref[...] + centre_ref[...]).astype(jnp.bfloat16)
    width = heads * SUBSPACE_WIDTH
    raw = dot(w_ref[...], normed, 1, 1)
    out_ref[:width, :] = (raw[:width] * SUBSPACE_WIDTH ** (-0.5)).astype(jnp.bfloat16)
    out_ref[width:, :] = raw[width:].astype(jnp.bfloat16)
    gate_ref[...] = jax.nn.sigmoid(dot(normed, wg_ref[...], 1, 0) + shift_ref[...])


def project_rows(rows, gain, centre, stacked, gate_weight, shift, heads):
    count, residues, channels = rows.shape
    width = heads * SUBSPACE_WIDTH
    full = lambda *shape: pl.BlockSpec(shape, lambda s: (0,) * len(shape))
    return pl.pallas_call(
        lambda *refs: rows_kernel(heads, *refs),
        grid=(count,),
        in_specs=[
            pl.BlockSpec((None, residues, channels), lambda s: (s, 0, 0)),
            full(1, channels),
            full(1, channels),
            full(3 * width, channels),
            full(channels, width),
            full(1, width),
        ],
        out_specs=[
            pl.BlockSpec((None, 3 * width, residues), lambda s: (s, 0, 0)),
            pl.BlockSpec((None, residues, width), lambda s: (s, 0, 0)),
        ],
        out_shape=[
            jax.ShapeDtypeStruct((count, 3 * width, residues), jnp.bfloat16),
            jax.ShapeDtypeStruct((count, residues, width), jnp.float32),
        ],
        cost_estimate=pl.CostEstimate(
            flops=30 * rows.size * 4 * width, bytes_accessed=14 << 20, transcendentals=0
        ),
        compiler_params=params(),
        name="row_projection",
    )(rows, gain[None], centre[None], stacked, gate_weight, shift[None])


def block_order(coords, sizes, relative):
    z, x, c = (lax.rem(coords[k] + relative[k], sizes[k]) for k in range(3))
    return (z * sizes[1] + x) * sizes[2] + c


def attention_kernel(
    tile, sizes, parts, head, at_ref, q_ref, k_ref, v_ref, gate_ref, gd_ref, *refs
):
    zs, xs, cs = sizes
    bias_parts, refs = refs[:cs], refs[cs:]
    grads_out, refs = refs[:parts], refs[parts:]
    sum_out, (bias_ref, acc_ref, grads_ref) = refs[:cs], refs[cs:]
    score_scale = SUBSPACE_WIDTH ** (-0.5)
    residues = acc_ref.shape[0]
    span = residues // (zs * xs * cs)
    group = span // PACK
    coords = [at_ref[k] for k in range(3)]
    places = [
        (c, x, z, pl.multiple_of(block_order(coords, sizes, (z, x, c)) * span, span))
        for c in range(cs)
        for x in range(xs)
        for z in range(zs)
    ]

    @pl.when(pl.program_id(0) == 0)
    def _():
        acc_ref[...] = jnp.zeros_like(acc_ref)
        for c, x, z, start in places:
            bias_ref[pl.ds(start, span), :] = bias_parts[c][x, z]

    keys_t = k_ref[...]
    vals_t = v_ref[...]
    key_grad = jnp.zeros((SUBSPACE_WIDTH, residues), jnp.float32)
    value_grad = jnp.zeros((SUBSPACE_WIDTH, residues), jnp.float32)
    lanes = slice(head * SUBSPACE_WIDTH, (head + 1) * SUBSPACE_WIDTH)
    for start in range(0, residues, tile):
        rows = slice(start, start + tile)
        query_t = q_ref[:, rows]
        query = query_t.astype(jnp.float32).T.astype(jnp.bfloat16)
        logits = dot(query, keys_t, 1, 0) + bias_ref[rows, :].astype(jnp.float32)
        top = jnp.max(logits, axis=-1, keepdims=True)
        weights = jnp.exp(logits - top)
        share = 1.0 / jnp.sum(weights, axis=-1, keepdims=True)
        weights_low = weights.astype(jnp.bfloat16)
        attended = dot(weights_low, vals_t, 1, 1) * share
        gate = gate_ref[rows, lanes]
        packed = gd_ref[start // PACK : (start + tile) // PACK, :].astype(jnp.float32)
        grad = jnp.concatenate(
            [
                packed[b * group : (b + 1) * group, k * SUBSPACE_WIDTH : (k + 1) * SUBSPACE_WIDTH]
                for b in range(tile // span)
                for k in range(PACK)
            ],
            axis=0,
        )
        out_grad = (grad * gate).astype(jnp.bfloat16).astype(jnp.float32)
        scaled = out_grad * share
        inner = jnp.sum(scaled * attended, axis=-1, keepdims=True)
        prob_grad = dot(scaled.astype(jnp.bfloat16), vals_t, 1, 0)
        score_grad = weights * (prob_grad - inner)
        acc_ref[rows, :] += score_grad
        score_low = score_grad.astype(jnp.bfloat16)
        query_grad = score_scale * dot(score_low, keys_t, 1, 1)
        key_grad += dot(query_t, score_low, 1, 0)
        value_grad += dot(scaled.T.astype(jnp.bfloat16), weights_low, 1, 0)
        gate_grad = grad * attended * gate * (1.0 - gate)
        grads_ref[0, :, rows] = query_grad.T.astype(jnp.bfloat16)
        grads_ref[3, :, rows] = gate_grad.T.astype(jnp.bfloat16)
    grads_ref[1] = key_grad.astype(jnp.bfloat16)
    grads_ref[2] = value_grad.astype(jnp.bfloat16)
    length = residues // parts
    for k in range(parts):
        begin = pl.multiple_of(lax.rem(at_ref[3] + k, parts) * length, length)
        for which in range(4):
            grads_out[k][which * SUBSPACE_WIDTH : (which + 1) * SUBSPACE_WIDTH, :] = grads_ref[
                which, :, pl.ds(begin, length)
            ]

    @pl.when(pl.program_id(0) == pl.num_programs(0) - 1)
    def _():
        for c, x, z, start in places:
            sum_out[c][x, z] = acc_ref[pl.ds(start, span), :].astype(jnp.bfloat16)


def attention_reverse(head, at, sizes, parts, projected, gate, gated_grad, bias_parts):
    rows, _, _, width, residues = projected.shape
    zs, xs, cs = sizes
    span = residues // (zs * xs * cs)
    tile = 256

    def part(which):
        return pl.BlockSpec(
            (None, None, None, width, residues), lambda s, at: (s, which, head, 0, 0)
        )

    row = lambda a: pl.BlockSpec((None,) + a.shape[1:], lambda s, at: (s, 0, 0))
    pieces = pl.BlockSpec((xs, zs, span, residues), lambda s, at: (0, 0, 0, 0))
    place, bias_parts = bias_parts
    bias_block = pl.BlockSpec(
        (xs, zs, None, span, residues), lambda s, at: (0, 0, place, 0, 0)
    )
    square = rows * residues * residues
    length = residues // parts
    outs = pl.pallas_call(
        lambda *refs: attention_kernel(tile, sizes, parts, head, *refs),
        grid_spec=pltpu.PrefetchScalarGridSpec(
            num_scalar_prefetch=1,
            grid=(rows,),
            in_specs=[part(0), part(1), part(2), row(gate), row(gated_grad)] + [bias_block] * cs,
            out_specs=[pl.BlockSpec((None, 4 * width, length), lambda s, at: (s, 0, 0))] * parts
            + [pieces] * cs,
            scratch_shapes=[
                pltpu.VMEM((residues, residues), jnp.bfloat16),
                pltpu.VMEM((residues, residues), jnp.float32),
                pltpu.VMEM((4, width, residues), jnp.bfloat16),
            ],
        ),
        out_shape=[jax.ShapeDtypeStruct((rows, 4 * width, length), jnp.bfloat16)] * parts
        + [jax.ShapeDtypeStruct((xs, zs, span, residues), jnp.bfloat16)] * cs,
        cost_estimate=pl.CostEstimate(
            flops=5500 * square, bytes_accessed=12 << 20, transcendentals=square
        ),
        compiler_params=params(),
    )(at, projected, projected, projected, gate, gated_grad, *bias_parts)
    return outs[:parts], outs[parts:]


def final_kernel(count, at_ref, x_ref, gain_ref, w_ref, *refs):
    grad_refs, out_ref = refs[:count], refs[count]
    width = grad_refs[0].shape[0]
    total = None
    for k in range(count):
        term = dot(grad_refs[k][...], w_ref[k * width : (k + 1) * width, :], 0, 0)
        total = term if total is None else total + term
    hat, inverse = layer_statistics(x_ref[...].astype(jnp.float32))
    out_ref[...] = layer_reverse_step(total * gain_ref[...], hat, inverse).astype(jnp.bfloat16)


def final_rows(at, rows, gain, weight, grads):
    count, width, length = grads[0].shape
    channels = rows.shape[-1]
    block = lambda s, at: (s, at[3], 0)
    return pl.pallas_call(
        lambda *refs: final_kernel(len(grads), *refs),
        grid_spec=pltpu.PrefetchScalarGridSpec(
            num_scalar_prefetch=1,
            grid=(count,),
            in_specs=[
                pl.BlockSpec((None, length, channels), block),
                pl.BlockSpec((1, channels), lambda s, at: (0, 0)),
                pl.BlockSpec(weight.shape, lambda s, at: (0, 0)),
            ]
            + [pl.BlockSpec((None, width, length), lambda s, at: (s, 0, 0))] * len(grads),
            out_specs=pl.BlockSpec((None, length, channels), lambda s, at: (s, 0, 0)),
        ),
        out_shape=jax.ShapeDtypeStruct((count, length, channels), jnp.bfloat16),
        cost_estimate=pl.CostEstimate(
            flops=4 * count * width * length * channels * len(grads),
            bytes_accessed=12 << 20,
            transcendentals=0,
        ),
        compiler_params=params(),
        name="final_rows",
    )(at, rows, gain[None], weight, *grads)


def pair_kernel(pair_ref, gain_ref, w_ref, bias_ref, out_ref):
    for i in range(pair_ref.shape[0]):
        upstream = dot(bias_ref[:, i, :], w_ref[...], 0, 0) * gain_ref[...]
        hat, inverse = layer_statistics(pair_ref[i].astype(jnp.float32))
        out_ref[i] = layer_reverse_step(upstream, hat, inverse).astype(jnp.bfloat16)


def pair_reverse(pair, gain, weight, bias):
    count, length, channels = pair.shape
    heads = bias.shape[0]
    block = 8
    return pl.pallas_call(
        pair_kernel,
        grid=(count // block,),
        in_specs=[
            pl.BlockSpec((block, length, channels), lambda s: (s, 0, 0)),
            pl.BlockSpec((1, channels), lambda s: (0, 0)),
            pl.BlockSpec((heads, channels), lambda s: (0, 0)),
            pl.BlockSpec((heads, block, length), lambda s: (0, s, 0)),
        ],
        out_specs=pl.BlockSpec((block, length, channels), lambda s: (s, 0, 0)),
        out_shape=jax.ShapeDtypeStruct(pair.shape, jnp.bfloat16),
        cost_estimate=pl.CostEstimate(
            flops=40 * pair.size, bytes_accessed=18 << 20, transcendentals=0
        ),
        compiler_params=params(),
        name="pair_reverse",
    )(pair, gain[None], weight, bias)


def stage_sizes(seq):
    cs = 2 if seq % 2 == 0 else 1
    rest = seq // cs
    xs = 1
    while rest % (xs * 2) == 0 and (xs * 2) * (xs * 2) <= rest:
        xs *= 2
    return rest // xs, xs, cs


def shift(value, sizes, which, step):
    zs, xs, cs = sizes
    pairs = []
    for z in range(zs):
        for x in range(xs):
            for c in range(cs):
                goal = [z, x, c]
                goal[which] = (goal[which] + step) % sizes[which]
                pairs.append(((z * xs + x) * cs + c, (goal[0] * xs + goal[1]) * cs + goal[2]))
    return lax.ppermute(value, "seq", pairs)


def gather_stage(value, sizes, which):
    return [value] + [
        shift(value, sizes, which, sizes[which] - step)
        for step in range(1, sizes[which])
    ]


def add(terms):
    total = terms[0].astype(jnp.float32)
    for term in terms[1:]:
        total = total + term.astype(jnp.float32)
    return total.astype(jnp.bfloat16)


def reduce_stage(pieces, sizes, which):
    return add(
        [pieces[0]]
        + [shift(pieces[step], sizes, which, step) for step in range(1, sizes[which])]
    )


def groups_of(heads):
    gathers = [[0], [1], list(range(2, heads))] if heads > 2 else [[h] for h in range(heads)]
    reduces = [list(range(heads - 2)), [heads - 2], [heads - 1]] if heads > 2 else gathers
    return gathers, reduces


def per_device(
    sizes,
    parts,
    alignment_rows,
    upstream_derivative_tensor,
    saved_pair_bias,
    pairwise_features,
    sequence_layernorm_scaling,
    sequence_layernorm_centre,
    asking_projection_matrix,
    matching_projection_matrix,
    content_projection_matrix,
    sigmoid_projection_matrix,
    gate_offset_bias,
    final_projection_matrix,
    pairwise_norm_gain,
    pairwise_weight,
):
    heads = saved_pair_bias.shape[0]
    all_heads = pairwise_weight.shape[1]
    count, residues, channels = alignment_rows.shape
    width = heads * SUBSPACE_WIDTH
    zs, xs, cs = sizes
    me = lax.axis_index("seq")
    part = lax.axis_index("head")
    at = jnp.stack([me // (xs * cs), (me // cs) % xs, me % cs, part]).astype(jnp.int32)
    first_col = part * width
    local = lambda matrix: lax.dynamic_slice_in_dim(matrix, first_col, width, 1)
    gathers, reduces = groups_of(heads)

    biases = [None] * heads
    for group in gathers:
        low = saved_pair_bias[group[0] : group[-1] + 1]
        low = jnp.stack(gather_stage(low, sizes, 0))
        wide = jnp.stack(gather_stage(low, sizes, 1))
        both = gather_stage(wide, sizes, 2)
        for place, head in enumerate(group):
            biases[head] = (place, both)
    out_rows = lax.dynamic_slice_in_dim(final_projection_matrix, first_col, width, 0)
    projected_up = project_upstream(upstream_derivative_tensor, out_rows, heads)
    gated = []
    for value in projected_up:
        gated.append(lax.all_to_all(value, "seq", split_axis=0, concat_axis=1, tiled=True))
    stacked = jnp.concatenate(
        [
            local(asking_projection_matrix),
            local(matching_projection_matrix),
            local(content_projection_matrix),
        ],
        axis=1,
    ).T
    projected, gate = project_rows(
        alignment_rows,
        sequence_layernorm_scaling,
        sequence_layernorm_centre,
        stacked,
        local(sigmoid_projection_matrix),
        lax.dynamic_slice_in_dim(gate_offset_bias, first_col, width, 0),
        heads,
    )
    projected = projected.reshape(count, 3, heads, SUBSPACE_WIDTH, residues)

    ring = lambda step: [(k, (k + step) % parts) for k in range(parts)]
    length = residues // parts
    grads = [[None] * heads for _ in range(parts)]
    chips = []
    for head in range(heads):
        split, pieces = attention_reverse(
            head, at, sizes, parts, projected, gate, gated[head], biases[head]
        )
        grads[0][head] = split[0]
        for k in range(1, parts):
            grads[k][head] = lax.ppermute(split[k], "head", ring(k))
        chips.append(reduce_stage(pieces, sizes, 2))
    totals = []
    for group in reduces:
        line = reduce_stage(
            [jnp.stack([chips[h][k] for h in group], axis=1) for k in range(xs)], sizes, 1
        )
        totals.append(reduce_stage([line[k] for k in range(zs)], sizes, 0))
    totals = [jnp.concatenate(totals[:-1]), totals[-1]] if len(totals) > 1 else totals
    sums = [[] for _ in range(parts)]
    for total in totals:
        for k in range(parts):
            block = lax.dynamic_slice_in_dim(total, ((part + k) % parts) * length, length, 2)
            sums[k].append(lax.ppermute(block, "head", ring(k)) if k else block)

    piled = jnp.stack(
        [
            matrix.reshape(channels, all_heads, SUBSPACE_WIDTH)
            for matrix in (
                asking_projection_matrix,
                matching_projection_matrix,
                content_projection_matrix,
                sigmoid_projection_matrix,
            )
        ],
        axis=2,
    )
    order = (part - jnp.arange(parts)) % parts
    weight = piled.reshape(channels, parts, heads * 4 * SUBSPACE_WIDTH).transpose(1, 2, 0)
    weight = weight[order].reshape(all_heads * 4 * SUBSPACE_WIDTH, channels)
    alignment_input_gradient = final_rows(
        at,
        alignment_rows,
        sequence_layernorm_scaling,
        weight,
        [g for group in grads for g in group],
    )
    pair_weight = pairwise_weight.T.reshape(parts, heads, -1)[order].reshape(all_heads, -1)
    pairwise_gradient = pair_reverse(
        pairwise_features,
        pairwise_norm_gain,
        pair_weight,
        jnp.concatenate([s for group in sums for s in group]),
    )
    return (alignment_input_gradient, pairwise_gradient)


def solution(mesh):
    placed = (
        P("seq", None, None),
        P(None, "seq", None),
        P("head", "seq", None),
        P("seq", "head", None),
    ) + (P(),) * 10
    sizes = stage_sizes(mesh.shape["seq"])
    parts = mesh.shape["head"]

    def body(*arrays):
        return per_device(sizes, parts, *arrays)

    return jax.shard_map(
        body,
        mesh=mesh,
        in_specs=placed,
        out_specs=(P("seq", "head", None), P("seq", "head", None)),
        check_vma=False,
    )
```

time: 576 us -> 478 us (0.83)
  waiting for transfers between devices: 234 us -> 115 us
  starting transfers between devices: 11.3 us -> 89.3 us
  Pallas kernels: 156 us -> 227 us
  local copies, waits for them, and re-layouts: 79.9 us -> 17.7 us
  other arithmetic: 54.6 us -> 21.8 us
  matrix products: 17.6 us -> 0 us
  between operations: 14.9 us -> 1.19 us
    reduce_scatter x5 -> x0, waiting for transfers between devices: 159 us -> none  [the longest x4 150 us: per_device(): lax.psum_scatter(bias_grad, 'seq', scatter_dimension=0, tiled=True)]
    ppermute x0 -> x37, waiting for transfers between devices: none -> 98.9 us  [the longest x4 60.7 us: per_device(): grads[k][head] = lax.ppermute(split[k], 'head', ring(k))]
    pallas_call x4 -> x8, Pallas kernels: 156 us -> 227 us  [the longest x4 175 us: attention_reverse(): pl.pallas_call(lambda *refs: attention_kernel(tile, sizes, parts, head, *...]
    ppermute x0 -> x37, starting transfers between devices: none -> 71.2 us  [the longest x31 65.1 us: shift(): return lax.ppermute(value, 'seq', pairs)]
    unnamed x76 -> x50, local copies, waits for them, and re-layouts: 58.9 us -> 0.5 us
    all_to_all x2 -> x4, waiting for transfers between devices: 72.6 us -> 15.9 us  [per_device(): lax.all_to_all(value, 'seq', split_axis=0, concat_axis=1, tiled=True)]
    reduce_sum x5 -> x0, other arithmetic: 20.5 us -> none  [the longest x2 9.45 us: layer_statistics(): average = jnp.mean(values, axis=-1, keepdims=True)]
    dot_general x4 -> x0, matrix products: 17.6 us -> none  [the longest x1 7.69 us: per_device(): jnp.einsum('hij,ch->ijc', bias_low, pairwise_weight, preferred_element_ty...]
  transfers between devices with their start and end apart: 11 -> 41, of which waited for: 6 -> 14; matrix products, arithmetic and copies ran while one was open for 19% -> 8% of each run, Pallas kernels for 27% -> 43%
where the time goes in v1:
time: 478 us; the launch traced here: 472 us
  Pallas kernels  227 us (47%)
  waiting for transfers between devices  115 us (24%)
  starting transfers between devices  89.3 us (19%)
  other arithmetic  21.8 us (5%)
  local copies, waits for them, and re-layouts  17.7 us (4%)
    pallas_call x4, Pallas kernels, attention_reverse(): pl.pallas_call(lambda *refs: attention_kernel(tile, sizes, parts, head, *...  175 us
    ppermute x31, starting transfers between devices, shift(): return lax.ppermute(value, 'seq', pairs)  65.1 us
    ppermute x4, waiting for transfers between devices, per_device(): grads[k][head] = lax.ppermute(split[k], 'head', ring(k))  60.7 us
    ppermute x31, waiting for transfers between devices, shift(): return lax.ppermute(value, 'seq', pairs)  38.1 us
    pallas_call x1, Pallas kernels, pair_reverse(): pl.pallas_call(pair_kernel, grid=(count // block,), in_specs=[pl.BlockSpe...  23.4 us
    all_to_all x4, starting transfers between devices, per_device(): lax.all_to_all(value, 'seq', split_axis=0, concat_axis=1, tiled=True)  18 us
    all_to_all x4, waiting for transfers between devices, per_device(): lax.all_to_all(value, 'seq', split_axis=0, concat_axis=1, tiled=True)  15.9 us
    convert_element_type x10, other arithmetic, add(): return total.astype(jnp.bfloat16)  12.3 us
  transfers between devices with their start and end apart: 41, of which 14 were waited for; matrix products, arithmetic and copies ran while one was open for 8% of the time, Pallas kernels for 43%

profile of v1, /device:TPU:0, one launch (start us, length us, event | category | flops | bytes accessed | tf_op | source)
XLA Modules:
  0.0 471.9 jit_solution(11874903228544565679)
XLA Ops:
  0.6 1.8 slice_bitcast_fusion.22
  2.4 5.1 %collective-permute-start.10 = (bf16[2,64,1024]{2,1,0:T(8,128)(2,1)}, bf16[2,64,1024]{2,1,0:T(8,128)(2,1)S(1)}, u32[]{:S(2)}, u32[]{:S(2)}) collective-permute-start(bf16[2,64,1024]{2,1,0:T(8,128)(2,1)} %get-tuple-element.62), channel_id=1, source_target_pairs={{0,24},{2,26},{4,28},{6,30},{8,0},{10,2},{12,4},{14,6},{16,8},{18,... | collective-permute-start | bytes 786440 | tf_op jit(solution)/shard_map/ppermute | solution.py:333
  7.5 1.7 slice_bitcast_fusion.20
  9.6 2.5 collective-permute-start.6
  12.1 2.0 collective-permute-start.7
  15.6 6.0 %upstream_projection.1 = (bf16[128,16,128]{2,1,0:T(8,128)(2,1)}, bf16[128,16,128]{2,1,0:T(8,128)(2,1)}, bf16[128,16,128]{2,1,0:T(8,128)(2,1)}, bf16[128,16,128]{2,1,0:T(8,128)(2,1)}) custom-call(bf16[128,64,256]{2,1,0:T(8,128)(2,1)} %refs_0_.3, bf16[4,256,512]{2,1,0:T(8,128)(2,1)} %copy.43.refs_1_), custom_call_target="tpu_custom_call" | custom-call | flops 2147483648 | bytes 8388608 | tf_op jit(solution)/shard_map/upstream_projection/pallas_call | solution.py:61
  21.7 4.3 all-to-all-start.1
  26.4 3.8 collective-permute-start
  30.1 12.2 %collective-permute-done.6 = bf16[1,64,1024]{2,1,0:T(8,128)(2,1)S(1)} collective-permute-done((bf16[1,64,1024]{2,1,0:T(8,128)(2,1)}, bf16[1,64,1024]{2,1,0:T(8,128)(2,1)S(1)}, u32[]{:S(2)}, u32[]{:S(2)}) %collective-permute-start.6) | collective-permute-done | bytes 131104 | tf_op jit(solution)/shard_map/ppermute | solution.py:333
  44.8 15.0 %collective-permute-start.12 = (bf16[2,64,1024]{2,1,0:T(8,128)(2,1)}, bf16[2,64,1024]{2,1,0:T(8,128)(2,1)S(1)}, u32[]{:S(2)}, u32[]{:S(2)}) collective-permute-start(bf16[2,64,1024]{2,1,0:T(8,128)(2,1)} %get-tuple-element.62), channel_id=1, source_target_pairs={{0,8},{2,10},{4,12},{6,14},{8,16},{10,18},{12,20},{14,22},{16,24},... | collective-permute-start | bytes 786440 | tf_op jit(solution)/shard_map/ppermute | solution.py:333
  62.3 5.4 %collective-permute-done.2 = bf16[1,64,1024]{2,1,0:T(8,128)(2,1)S(1)} collective-permute-done((bf16[1,64,1024]{2,1,0:T(8,128)(2,1)S(1)}, bf16[1,64,1024]{2,1,0:T(8,128)(2,1)S(1)}, u32[]{:S(2)}, u32[]{:S(2)}) %collective-permute-start.2) | collective-permute-done | bytes 131104 | tf_op jit(solution)/shard_map/ppermute | solution.py:333
  69.3 2.1 fusion.19
  73.1 3.6 all-to-all-start
  76.7 10.7 %row_projection.1 = (bf16[8,384,1024]{2,1,0:T(8,128)(2,1)}, f32[8,1024,128]{2,1,0:T(8,128)}) custom-call(bf16[8,1024,256]{2,1,0:T(8,128)(2,1)} %refs_1_.1, f32[1,256]{1,0:T(1,128)} %bitcast.177, f32[1,256]{1,0:T(1,128)} %bitcast.176, bf16[384,256]{1,0:T(8,128)(2,1)} %maximum_bitcast_fusion.refs_3_, bf16[256,128]{1,0:T(8,128)(2,1)} %constant_dynamic-slice_fusion.3.refs_4_, ...), custom_call_target="tpu_custom_call" | custom-call | flops 32212254720 | bytes 14680064 | tf_op jit(solution)/shard_map/row_projection/pallas_call | solution.py:92
  88.0 2.1 pad_maximum_fusion.1.refs_6_
  91.4 15.9 %all-to-all-done = bf16[128,16,128]{2,1,0:T(8,128)(2,1)S(1)} async-done(((bf16[128,16,128]{2,1,0:T(8,128)(2,1)}), bf16[128,16,128]{2,1,0:T(8,128)(2,1)S(1)}, u32[]{:S(2)}, u32[]{:S(2)}) %all-to-all-start) | async-done | bytes 524320 | tf_op jit(solution)/shard_map/all_to_all | solution.py:405
  107.2 4.2 all-to-all-start.2
  114.1 43.8 %shard_map.150 = (bf16[8,128,512]{2,1,0:T(8,128)(2,1)}, bf16[8,128,512]{2,1,0:T(8,128)(2,1)}, bf16[2,4,64,1024]{3,2,1,0:T(8,128)(2,1)}, bf16[2,4,64,1024]{3,2,1,0:T(8,128)(2,1)}) custom-call(s32[4]{0:T(128)} %pad_add_fusion.refs_0_, bf16[8,3,4,32,1024]{4,3,2,1,0:T(8,128)(2,1)} %bitcast.179, bf16[8,3,4,32,1024]{4,3,2,1,0:T(8,128)(2,1)} %bitcast.180, ...), custom_call_target="tpu_custom_call" | custom-call | flops 46137344000 | bytes 12582912 | tf_op jit(solution)/shard_map/pallas_call | solution.py:222
  158.2 5.9 %all-to-all-start.3 = ((bf16[128,16,128]{2,1,0:T(8,128)(2,1)}), bf16[128,16,128]{2,1,0:T(8,128)(2,1)S(1)}, u32[]{:S(2)}, u32[]{:S(2)}) async-start(bf16[128,16,128]{2,1,0:T(8,128)(2,1)} %get-tuple-element.32), calls=%async_computation.3 | async-start | bytes 1048576 | tf_op jit(solution)/shard_map/all_to_all | solution.py:405
  164.1 43.8 %shard_map.149 = (bf16[8,128,512]{2,1,0:T(8,128)(2,1)}, bf16[8,128,512]{2,1,0:T(8,128)(2,1)}, bf16[2,4,64,1024]{3,2,1,0:T(8,128)(2,1)}, bf16[2,4,64,1024]{3,2,1,0:T(8,128)(2,1)}) custom-call(s32[4]{0:T(128)} %pad_add_fusion.refs_0_, bf16[8,3,4,32,1024]{4,3,2,1,0:T(8,128)(2,1)} %bitcast.182, bf16[8,3,4,32,1024]{4,3,2,1,0:T(8,128)(2,1)} %bitcast.183, ...), custom_call_target="tpu_custom_call" | custom-call | flops 46137344000 | bytes 12582912 | tf_op jit(solution)/shard_map/pallas_call | solution.py:222
  208.3 1.9 copy.54
  211.1 2.0 add_convert_fusion.2
  214.0 1.6 add_convert_fusion.3
  216.6 1.7 collective-permute-start.21
  218.3 43.6 %shard_map.151 = (bf16[8,128,512]{2,1,0:T(8,128)(2,1)}, bf16[8,128,512]{2,1,0:T(8,128)(2,1)}, bf16[2,4,64,1024]{3,2,1,0:T(8,128)(2,1)}, bf16[2,4,64,1024]{3,2,1,0:T(8,128)(2,1)}) custom-call(s32[4]{0:T(128)} %pad_add_fusion.refs_0_, bf16[8,3,4,32,1024]{4,3,2,1,0:T(8,128)(2,1)} %bitcast.185, bf16[8,3,4,32,1024]{4,3,2,1,0:T(8,128)(2,1)} %bitcast.186, ...), custom_call_target="tpu_custom_call" | custom-call | flops 46137344000 | bytes 12582912 | tf_op jit(solution)/shard_map/pallas_call | solution.py:222
  262.2 44.0 %shard_map.152 = (bf16[8,128,512]{2,1,0:T(8,128)(2,1)}, bf16[8,128,512]{2,1,0:T(8,128)(2,1)}, bf16[2,4,64,1024]{3,2,1,0:T(8,128)(2,1)}, bf16[2,4,64,1024]{3,2,1,0:T(8,128)(2,1)}) custom-call(s32[4]{0:T(128)} %pad_add_fusion.refs_0_, bf16[8,3,4,32,1024]{4,3,2,1,0:T(8,128)(2,1)} %bitcast.188, bf16[8,3,4,32,1024]{4,3,2,1,0:T(8,128)(2,1)} %bitcast.189, ...), custom_call_target="tpu_custom_call" | custom-call | flops 46137344000 | bytes 12582912 | tf_op jit(solution)/shard_map/pallas_call | solution.py:222
  306.9 1.7 fusion
  308.7 1.7 add_convert_fusion.1
  310.9 1.6 add_convert_fusion
  312.6 1.7 collective-permute-start.31
  316.5 2.4 collective-permute-start.23
  320.3 5.0 %collective-permute-done.26 = bf16[4,1,64,1024]{3,2,1,0:T(8,128)(2,1)S(1)} collective-permute-done((bf16[4,1,64,1024]{3,2,1,0:T(8,128)(2,1)S(1)}, bf16[4,1,64,1024]{3,2,1,0:T(8,128)(2,1)S(1)}, u32[]{:S(2)}, u32[]{:S(2)}) %collective-permute-start.26) | collective-permute-done | bytes 524320 | tf_op jit(solution)/shard_map/ppermute | solution.py:333
  327.7 8.0 %collective-permute-done.31 = bf16[4,1,64,1024]{3,2,1,0:T(8,128)(2,1)S(1)} collective-permute-done((bf16[4,1,64,1024]{3,2,1,0:T(8,128)(2,1)S(1)}, bf16[4,1,64,1024]{3,2,1,0:T(8,128)(2,1)S(1)}, u32[]{:S(2)}, u32[]{:S(2)}) %collective-permute-start.31) | collective-permute-done | bytes 524320 | tf_op jit(solution)/shard_map/ppermute | solution.py:333
  335.7 2.4 collective-permute-start.28
  340.6 6.6 %collective-permute-start.32 = (bf16[1,64,1024]{2,1,0:T(8,128)(2,1)}, bf16[1,64,1024]{2,1,0:T(8,128)(2,1)}, u32[]{:S(2)}, u32[]{:S(2)}) collective-permute-start(bf16[1,64,1024]{2,1,0:T(8,128)(2,1)} %get-tuple-element.58), channel_id=1, source_target_pairs={{0,8},{2,10},{4,12},{6,14},{8,16},{10,18},{12,20},{14,22},{16,24},... | collective-permute-start | bytes 393224 | tf_op jit(solution)/shard_map/ppermute | solution.py:333
  347.3 1.7 collective-permute-start.16
  349.4 2.1 collective-permute-done.28
  351.5 1.6 collective-permute-start.18
  356.1 3.2 collective-permute-start.33
  360.5 2.4 collective-permute-done.33
  362.9 6.2 %collective-permute-start.34 = (bf16[1,64,1024]{2,1,0:T(8,128)(2,1)S(1)}, bf16[1,64,1024]{2,1,0:T(8,128)(2,1)S(1)}, u32[]{:S(2)}, u32[]{:S(2)}) collective-permute-start(bf16[1,64,1024]{2,1,0:T(8,128)(2,1)S(1)} %copy-done.20), channel_id=1, source_target_pairs={{0,24},{2,26},{4,28},{6,30},{8,0},{10,2},{12,4},{14,6},{16,8},{18,... | collective-permute-start | bytes 393224 | tf_op jit(solution)/shard_map/ppermute | solution.py:333
  370.2 1.7 collective-permute-done.34
  373.7 1.6 collective-permute-start.36
  375.3 20.9 %collective-permute-done.15.refs_8_ = bf16[8,128,512]{2,1,0:T(8,128)(2,1)} collective-permute-done((bf16[8,128,512]{2,1,0:T(8,128)(2,1)}, bf16[8,128,512]{2,1,0:T(8,128)(2,1)}, u32[]{:S(2)}, u32[]{:S(2)}) %collective-permute-start.15) | collective-permute-done | bytes 1048608 | tf_op jit(solution)/shard_map/ppermute | solution.py:435
  396.2 22.5 %collective-permute-done.18.refs_11_ = bf16[8,128,512]{2,1,0:T(8,128)(2,1)} collective-permute-done((bf16[8,128,512]{2,1,0:T(8,128)(2,1)}, bf16[8,128,512]{2,1,0:T(8,128)(2,1)}, u32[]{:S(2)}, u32[]{:S(2)}) %collective-permute-start.18) | collective-permute-done | bytes 1048608 | tf_op jit(solution)/shard_map/ppermute | solution.py:435
  418.6 17.0 %collective-permute-done.17.refs_10_ = bf16[8,128,512]{2,1,0:T(8,128)(2,1)} collective-permute-done((bf16[8,128,512]{2,1,0:T(8,128)(2,1)}, bf16[8,128,512]{2,1,0:T(8,128)(2,1)}, u32[]{:S(2)}, u32[]{:S(2)}) %collective-permute-start.17) | collective-permute-done | bytes 1048608 | tf_op jit(solution)/shard_map/ppermute | solution.py:435
  435.7 12.0 %final_rows.1 = bf16[8,512,256]{2,1,0:T(8,128)(2,1)} custom-call(s32[4]{0:T(128)} %pad_add_fusion.refs_0_, bf16[8,1024,256]{2,1,0:T(8,128)(2,1)} %refs_1_.1, f32[1,256]{1,0:T(1,128)} %bitcast.178, bf16[1024,256]{1,0:T(8,128)(2,1)} %bitcast.161, bf16[8,128,512]{2,1,0:T(8,128)(2,1)} %get-tuple-element.27.refs_4_, ...), custom_call_target="tpu_custom_call" | custom-call | flops 4294967296 | bytes 12582912 | tf_op jit(solution)/shard_map/final_rows/pallas_call | solution.py:261
  448.6 23.4 %pair_reverse.1 = bf16[64,512,128]{2,1,0:T(8,128)(2,1)} custom-call(bf16[64,512,128]{2,1,0:T(8,128)(2,1)} %pair_ref.1, f32[1,128]{1,0:T(1,128)} %bitcast.175, bf16[8,128]{1,0:T(8,128)(2,1)} %bitcast.173, bf16[8,64,512]{2,1,0:T(8,128)(2,1)} %pad_maximum_fusion.8.bias_ref), custom_call_target="tpu_custom_call" | custom-call | flops 167772160 | bytes 18874368 | tf_op jit(solution)/shard_map/pair_reverse/pallas_call | solution.py:296
  (141 shorter events, 36.8 us)
Async XLA Ops:
  2.4 66.9 %collective-permute-start.10 = (bf16[2,64,1024]{2,1,0:T(8,128)(2,1)}, bf16[2,64,1024]{2,1,0:T(8,128)(2,1)S(1)}, u32[]{:S(2)}, u32[]{:S(2)}) collective-permute-start(bf16[2,64,1024]{2,1,0:T(8,128)(2,1)} %get-tuple-element.62), channel_id=1, source_target_pairs={{0,24},{2,26},{4,28},{6,30},{8,0},{10,2},{12,4},{14,6},{16,8},{18,... | collective-permute-start | bytes 786440 | tf_op jit(solution)/shard_map/ppermute | solution.py:333
  7.5 61.9 %collective-permute-start.11 = (bf16[2,64,1024]{2,1,0:T(8,128)(2,1)}, bf16[2,64,1024]{2,1,0:T(8,128)(2,1)}, u32[]{:S(2)}, u32[]{:S(2)}) collective-permute-start(bf16[2,64,1024]{2,1,0:T(8,128)(2,1)} %get-tuple-element.62), channel_id=1, source_target_pairs={{0,16},{2,18},{4,20},{6,22},{8,24},{10,26},{12,28},{14,30},{16,0},... | collective-permute-start | bytes 786440 | tf_op jit(solution)/shard_map/ppermute | solution.py:333
  9.2 17.2 %collective-permute-start.5 = (bf16[1,64,1024]{2,1,0:T(8,128)(2,1)}, bf16[1,64,1024]{2,1,0:T(8,128)(2,1)S(1)}, u32[]{:S(2)}, u32[]{:S(2)}) collective-permute-start(bf16[1,64,1024]{2,1,0:T(8,128)(2,1)} %get-tuple-element.68), channel_id=1, source_target_pairs={{0,24},{2,26},{4,28},{6,30},{8,0},{10,2},{12,4},{14,6},{16,8},{18,... | collective-permute-start | bytes 393224 | tf_op jit(solution)/shard_map/ppermute | solution.py:333
  9.6 32.7 %collective-permute-start.6 = (bf16[1,64,1024]{2,1,0:T(8,128)(2,1)}, bf16[1,64,1024]{2,1,0:T(8,128)(2,1)S(1)}, u32[]{:S(2)}, u32[]{:S(2)}) collective-permute-start(bf16[1,64,1024]{2,1,0:T(8,128)(2,1)} %get-tuple-element.68), channel_id=1, source_target_pairs={{0,16},{2,18},{4,20},{6,22},{8,24},{10,26},{12,28},{14,30},{16,0},... | collective-permute-start | bytes 393224 | tf_op jit(solution)/shard_map/ppermute | solution.py:333
  12.1 30.3 %collective-permute-start.7 = (bf16[1,64,1024]{2,1,0:T(8,128)(2,1)}, bf16[1,64,1024]{2,1,0:T(8,128)(2,1)S(1)}, u32[]{:S(2)}, u32[]{:S(2)}) collective-permute-start(bf16[1,64,1024]{2,1,0:T(8,128)(2,1)} %get-tuple-element.68), channel_id=1, source_target_pairs={{0,8},{2,10},{4,12},{6,14},{8,16},{10,18},{12,20},{14,22},{16,24},... | collective-permute-start | bytes 393224 | tf_op jit(solution)/shard_map/ppermute | solution.py:333
  21.7 51.4 %all-to-all-start.1 = ((bf16[128,16,128]{2,1,0:T(8,128)(2,1)}), bf16[128,16,128]{2,1,0:T(8,128)(2,1)S(1)}, u32[]{:S(2)}, u32[]{:S(2)}) async-start(bf16[128,16,128]{2,1,0:T(8,128)(2,1)} %get-tuple-element.28), calls=%async_computation.1 | async-start | bytes 1048576 | tf_op jit(solution)/shard_map/all_to_all | solution.py:405
  26.4 18.5 %collective-permute-start = (bf16[1,64,1024]{2,1,0:T(8,128)(2,1)S(1)}, bf16[1,64,1024]{2,1,0:T(8,128)(2,1)S(1)}, u32[]{:S(2)}, u32[]{:S(2)}) collective-permute-start(bf16[1,64,1024]{2,1,0:T(8,128)(2,1)S(1)} %get-tuple-element.67), channel_id=1, source_target_pairs={{0,24},{2,26},{4,28},{6,30},{8,0},{10,2},{12,4},{14,6},{16,8},{18,... | collective-permute-start | bytes 393224 | tf_op jit(solution)/shard_map/ppermute | solution.py:333
  42.4 18.5 %collective-permute-start.1 = (bf16[1,64,1024]{2,1,0:T(8,128)(2,1)S(1)}, bf16[1,64,1024]{2,1,0:T(8,128)(2,1)S(1)}, u32[]{:S(2)}, u32[]{:S(2)}) collective-permute-start(bf16[1,64,1024]{2,1,0:T(8,128)(2,1)S(1)} %get-tuple-element.67), channel_id=1, source_target_pairs={{0,16},{2,18},{4,20},{6,22},{8,24},{10,26},{12,28},{14,30},{16,0},... | collective-permute-start | bytes 393224 | tf_op jit(solution)/shard_map/ppermute | solution.py:333
  42.5 29.5 %collective-permute-start.8 = (bf16[4,1,64,1024]{3,2,0,1:T(8,128)(2,1)S(1)}, bf16[4,1,64,1024]{3,2,0,1:T(8,128)(2,1)S(1)}, u32[]{:S(2)}, u32[]{:S(2)}) collective-permute-start(bf16[4,1,64,1024]{3,2,0,1:T(8,128)(2,1)S(1)} %get-tuple-element.64), channel_id=1, source_target_pairs={{0,4},{2,6},{4,0},{6,2},{8,12},{10,14},{12,8},{14,10},{16,20},{18,... | collective-permute-start | bytes 1572872 | tf_op jit(solution)/shard_map/ppermute | solution.py:333
  44.8 24.5 %collective-permute-start.12 = (bf16[2,64,1024]{2,1,0:T(8,128)(2,1)}, bf16[2,64,1024]{2,1,0:T(8,128)(2,1)S(1)}, u32[]{:S(2)}, u32[]{:S(2)}) collective-permute-start(bf16[2,64,1024]{2,1,0:T(8,128)(2,1)} %get-tuple-element.62), channel_id=1, source_target_pairs={{0,8},{2,10},{4,12},{6,14},{8,16},{10,18},{12,20},{14,22},{16,24},... | collective-permute-start | bytes 786440 | tf_op jit(solution)/shard_map/ppermute | solution.py:333
  60.9 6.8 %collective-permute-start.2 = (bf16[1,64,1024]{2,1,0:T(8,128)(2,1)S(1)}, bf16[1,64,1024]{2,1,0:T(8,128)(2,1)S(1)}, u32[]{:S(2)}, u32[]{:S(2)}) collective-permute-start(bf16[1,64,1024]{2,1,0:T(8,128)(2,1)S(1)} %get-tuple-element.67), channel_id=1, source_target_pairs={{0,8},{2,10},{4,12},{6,14},{8,16},{10,18},{12,20},{14,22},{16,24},... | collective-permute-start | bytes 393224 | tf_op jit(solution)/shard_map/ppermute | solution.py:333
  67.8 20.2 %collective-permute-start.3 = (bf16[4,1,64,1024]{3,2,0,1:T(8,128)(2,1)S(1)}, bf16[4,1,64,1024]{3,2,0,1:T(8,128)(2,1)}, u32[]{:S(2)}, u32[]{:S(2)}) collective-permute-start(bf16[4,1,64,1024]{3,2,0,1:T(8,128)(2,1)S(1)} %get-tuple-element.70), channel_id=1, source_target_pairs={{0,4},{2,6},{4,0},{6,2},{8,12},{10,14},{12,8},{14,10},{16,20},{18,... | collective-permute-start | bytes 1572872 | tf_op jit(solution)/shard_map/ppermute | solution.py:333
  71.4 40.9 %collective-permute-start.13 = (bf16[4,2,64,1024]{3,2,1,0:T(8,128)(2,1)}, bf16[4,2,64,1024]{3,2,1,0:T(8,128)(2,1)}, u32[]{:S(2)}, u32[]{:S(2)}) collective-permute-start(bf16[4,2,64,1024]{3,2,1,0:T(8,128)(2,1)} %get-tuple-element.54), channel_id=1, source_target_pairs={{0,4},{2,6},{4,0},{6,2},{8,12},{10,14},{12,8},{14,10},{16,20},{18,... | collective-permute-start | bytes 3145736 | tf_op jit(solution)/shard_map/ppermute | solution.py:333
  73.1 41.0 %collective-permute-start.9 = (bf16[2,4,1,64,1024]{4,3,2,1,0:T(8,128)(2,1)}, bf16[2,4,1,64,1024]{4,3,2,1,0:T(8,128)(2,1)}, u32[]{:S(2)}, u32[]{:S(2)}) collective-permute-start(bf16[2,4,1,64,1024]{4,3,2,1,0:T(8,128)(2,1)} %pad_maximum_fusion.2.refs_6_), channel_id=1, source_target_pairs={{0,2},{2,0},{4,6},{6,4},{8,10},{10,8},{12,14},{14,12},{16,18},{18,... | collective-permute-start | bytes 3145736 | tf_op jit(solution)/shard_map/ppermute | solution.py:333
  73.1 34.2 %all-to-all-start = ((bf16[128,16,128]{2,1,0:T(8,128)(2,1)}), bf16[128,16,128]{2,1,0:T(8,128)(2,1)S(1)}, u32[]{:S(2)}, u32[]{:S(2)}) async-start(bf16[128,16,128]{2,1,0:T(8,128)(2,1)} %get-tuple-element.26), calls=%async_computation | async-start | bytes 1048576 | tf_op jit(solution)/shard_map/all_to_all | solution.py:405
  90.1 74.0 %collective-permute-start.4 = (bf16[2,4,1,64,1024]{4,3,2,1,0:T(8,128)(2,1)}, bf16[2,4,1,64,1024]{4,3,2,1,0:T(8,128)(2,1)}, u32[]{:S(2)}, u32[]{:S(2)}) collective-permute-start(bf16[2,4,1,64,1024]{4,3,2,1,0:T(8,128)(2,1)} %pad_maximum_fusion.1.refs_6_), channel_id=1, source_target_pairs={{0,2},{2,0},{4,6},{6,4},{8,10},{10,8},{12,14},{14,12},{16,18},{18,... | collective-permute-start | bytes 3145736 | tf_op jit(solution)/shard_map/ppermute | solution.py:333
  107.2 50.9 %all-to-all-start.2 = ((bf16[128,16,128]{2,1,0:T(8,128)(2,1)}), bf16[128,16,128]{2,1,0:T(8,128)(2,1)}, u32[]{:S(2)}, u32[]{:S(2)}) async-start(bf16[128,16,128]{2,1,0:T(8,128)(2,1)} %get-tuple-element.30), calls=%async_computation.2 | async-start | bytes 1048576 | tf_op jit(solution)/shard_map/all_to_all | solution.py:405
  113.7 44.1 %copy-start.2 = (bf16[2,4,2,64,1024]{4,3,2,1,0:T(8,128)(2,1)}, bf16[2,4,2,64,1024]{4,3,2,1,0:T(8,128)(2,1)S(1)}, u32[]{:S(2)}) copy-start(bf16[2,4,2,64,1024]{4,3,2,1,0:T(8,128)(2,1)S(1)} %pad_maximum_fusion.refs_6_) | copy-start | bytes 6291460
  113.8 104.6 %collective-permute-start.14 = (bf16[2,4,2,64,1024]{4,3,2,1,0:T(8,128)(2,1)S(1)}, bf16[2,4,2,64,1024]{4,3,2,1,0:T(8,128)(2,1)}, u32[]{:S(2)}, u32[]{:S(2)}) collective-permute-start(bf16[2,4,2,64,1024]{4,3,2,1,0:T(8,128)(2,1)S(1)} %pad_maximum_fusion.refs_6_), channel_id=1, source_target_pairs={{0,2},{2,0},{4,6},{6,4},{8,10},{10,8},{12,14},{14,12},{16,18},{18,... | collective-permute-start | bytes 6291464 | tf_op jit(solution)/shard_map/ppermute | solution.py:333
  157.8 53.2 %collective-permute-start.20 = (bf16[2,4,64,1024]{3,2,1,0:T(8,128)(2,1)}, bf16[2,4,64,1024]{3,2,1,0:T(8,128)(2,1)}, u32[]{:S(2)}, u32[]{:S(2)}) collective-permute-start(bf16[2,4,64,1024]{3,2,1,0:T(8,128)(2,1)} %get-tuple-element.41), channel_id=1, source_target_pairs={{0,2},{2,0},{4,6},{6,4},{8,10},{10,8},{12,14},{14,12},{16,18},{18,... | collective-permute-start | bytes 3145736 | tf_op jit(solution)/shard_map/ppermute | solution.py:333
  158.2 52.0 %all-to-all-start.3 = ((bf16[128,16,128]{2,1,0:T(8,128)(2,1)}), bf16[128,16,128]{2,1,0:T(8,128)(2,1)S(1)}, u32[]{:S(2)}, u32[]{:S(2)}) async-start(bf16[128,16,128]{2,1,0:T(8,128)(2,1)} %get-tuple-element.32), calls=%async_computation.3 | async-start | bytes 1048576 | tf_op jit(solution)/shard_map/all_to_all | solution.py:405
  207.9 6.1 %collective-permute-start.19 = (bf16[2,4,64,1024]{3,2,1,0:T(8,128)(2,1)}, bf16[2,4,64,1024]{3,2,1,0:T(8,128)(2,1)}, u32[]{:S(2)}, u32[]{:S(2)}) collective-permute-start(bf16[2,4,64,1024]{3,2,1,0:T(8,128)(2,1)} %get-tuple-element.39), channel_id=1, source_target_pairs={{0,2},{2,0},{4,6},{6,4},{8,10},{10,8},{12,14},{14,12},{16,18},{18,... | collective-permute-start | bytes 3145736 | tf_op jit(solution)/shard_map/ppermute | solution.py:333
  216.6 90.3 %collective-permute-start.21 = (bf16[4,2,64,1024]{3,2,1,0:T(8,128)(2,1)S(1)}, bf16[4,2,64,1024]{3,2,1,0:T(8,128)(2,1)}, u32[]{:S(2)}, u32[]{:S(2)}) collective-permute-start(bf16[4,2,64,1024]{3,2,1,0:T(8,128)(2,1)S(1)} %pad_maximum_fusion.4), channel_id=1, source_target_pairs={{0,4},{2,6},{4,0},{6,2},{8,12},{10,14},{12,8},{14,10},{16,20},{18,... | collective-permute-start | bytes 3145736 | tf_op jit(solution)/shard_map/ppermute | solution.py:333
  262.0 46.7 %collective-permute-start.25 = (bf16[2,4,64,1024]{3,2,1,0:T(8,128)(2,1)}, bf16[2,4,64,1024]{3,2,1,0:T(8,128)(2,1)}, u32[]{:S(2)}, u32[]{:S(2)}) collective-permute-start(bf16[2,4,64,1024]{3,2,1,0:T(8,128)(2,1)} %get-tuple-element.43), channel_id=1, source_target_pairs={{0,2},{2,0},{4,6},{6,4},{8,10},{10,8},{12,14},{14,12},{16,18},{18,... | collective-permute-start | bytes 3145736 | tf_op jit(solution)/shard_map/ppermute | solution.py:333
  262.2 44.5 %copy-start.15 = (bf16[256,256]{1,0:T(8,128)(2,1)S(1)}, bf16[256,256]{1,0:T(8,128)(2,1)}, u32[]{:S(2)}) copy-start(bf16[256,256]{1,0:T(8,128)(2,1)} %param.23) | copy-start | bytes 393220
  262.2 44.6 %copy-start.9 = (bf16[256,256]{0,1:T(8,128)(2,1)S(1)}, bf16[256,256]{0,1:T(8,128)(2,1)}, u32[]{:S(2)}) copy-start(bf16[256,256]{0,1:T(8,128)(2,1)} %copy-done.8) | copy-start | bytes 393220
  262.2 44.6 %copy-start.11 = (bf16[256,256]{0,1:T(8,128)(2,1)S(1)}, bf16[256,256]{0,1:T(8,128)(2,1)}, u32[]{:S(2)}) copy-start(bf16[256,256]{0,1:T(8,128)(2,1)} %copy-done.10) | copy-start | bytes 393220
  262.2 44.6 %copy-start.13 = (bf16[256,256]{0,1:T(8,128)(2,1)S(1)}, bf16[256,256]{0,1:T(8,128)(2,1)}, u32[]{:S(2)}) copy-start(bf16[256,256]{0,1:T(8,128)(2,1)} %copy-done.12) | copy-start | bytes 393220
  262.2 44.7 %copy-start.3 = (bf16[4,1,64,1024]{3,2,0,1:T(8,128)(2,1)S(1)}, bf16[4,1,64,1024]{3,2,0,1:T(8,128)(2,1)}, u32[]{:S(2)}) copy-start(bf16[4,1,64,1024]{3,2,0,1:T(8,128)(2,1)} %get-tuple-element.52) | copy-start | bytes 1572868
  262.2 44.7 %copy-start.4 = (bf16[4,1,64,1024]{3,2,0,1:T(8,128)(2,1)S(1)}, bf16[4,1,64,1024]{3,2,0,1:T(8,128)(2,1)}, u32[]{:S(2)}) copy-start(bf16[4,1,64,1024]{3,2,0,1:T(8,128)(2,1)} %get-tuple-element.50) | copy-start | bytes 1572868
  306.2 4.7 collective-permute-start.30
  310.4 14.9 %collective-permute-start.26 = (bf16[4,1,64,1024]{3,2,1,0:T(8,128)(2,1)S(1)}, bf16[4,1,64,1024]{3,2,1,0:T(8,128)(2,1)S(1)}, u32[]{:S(2)}, u32[]{:S(2)}) collective-permute-start(bf16[4,1,64,1024]{3,2,1,0:T(8,128)(2,1)S(1)} %slice_bitcast_fusion.2), channel_id=1, source_target_pairs={{0,4},{2,6},{4,0},{6,2},{8,12},{10,14},{12,8},{14,10},{16,20},{18,... | collective-permute-start | bytes 1572872 | tf_op jit(solution)/shard_map/ppermute | solution.py:333
  312.6 23.1 %collective-permute-start.31 = (bf16[4,1,64,1024]{3,2,1,0:T(8,128)(2,1)S(1)}, bf16[4,1,64,1024]{3,2,1,0:T(8,128)(2,1)S(1)}, u32[]{:S(2)}, u32[]{:S(2)}) collective-permute-start(bf16[4,1,64,1024]{3,2,1,0:T(8,128)(2,1)S(1)} %slice_bitcast_fusion), channel_id=1, source_target_pairs={{0,4},{2,6},{4,0},{6,2},{8,12},{10,14},{12,8},{14,10},{16,20},{18,... | collective-permute-start | bytes 1572872 | tf_op jit(solution)/shard_map/ppermute | solution.py:333
  315.0 23.2 %collective-permute-start.22 = (bf16[2,64,1024]{2,1,0:T(8,128)(2,1)S(1)}, bf16[2,64,1024]{2,1,0:T(8,128)(2,1)S(1)}, u32[]{:S(2)}, u32[]{:S(2)}) collective-permute-start(bf16[2,64,1024]{2,1,0:T(8,128)(2,1)S(1)} %get-tuple-element.46), channel_id=1, source_target_pairs={{0,8},{2,10},{4,12},{6,14},{8,16},{10,18},{12,20},{14,22},{16,24},... | collective-permute-start | bytes 786440 | tf_op jit(solution)/shard_map/ppermute | solution.py:333
  316.5 24.1 %collective-permute-start.23 = (bf16[2,64,1024]{2,1,0:T(8,128)(2,1)S(1)}, bf16[2,64,1024]{2,1,0:T(8,128)(2,1)S(1)}, u32[]{:S(2)}, u32[]{:S(2)}) collective-permute-start(bf16[2,64,1024]{2,1,0:T(8,128)(2,1)S(1)} %get-tuple-element.48), channel_id=1, source_target_pairs={{0,16},{2,18},{4,20},{6,22},{8,24},{10,26},{12,28},{14,30},{16,0},... | collective-permute-start | bytes 786440 | tf_op jit(solution)/shard_map/ppermute | solution.py:333
  318.9 28.4 %collective-permute-start.24 = (bf16[2,64,1024]{2,1,0:T(8,128)(2,1)}, bf16[2,64,1024]{2,1,0:T(8,128)(2,1)}, u32[]{:S(2)}, u32[]{:S(2)}) collective-permute-start(bf16[2,64,1024]{2,1,0:T(8,128)(2,1)} %get-tuple-element.47), channel_id=1, source_target_pairs={{0,24},{2,26},{4,28},{6,30},{8,0},{10,2},{12,4},{14,6},{16,8},{18,... | collective-permute-start | bytes 786440 | tf_op jit(solution)/shard_map/ppermute | solution.py:333
  326.3 22.7 %collective-permute-start.27 = (bf16[1,64,1024]{2,1,0:T(8,128)(2,1)}, bf16[1,64,1024]{2,1,0:T(8,128)(2,1)S(1)}, u32[]{:S(2)}, u32[]{:S(2)}) collective-permute-start(bf16[1,64,1024]{2,1,0:T(8,128)(2,1)} %get-tuple-element.55), channel_id=1, source_target_pairs={{0,8},{2,10},{4,12},{6,14},{8,16},{10,18},{12,20},{14,22},{16,24},... | collective-permute-start | bytes 393224 | tf_op jit(solution)/shard_map/ppermute | solution.py:333
  335.7 15.8 %collective-permute-start.28 = (bf16[1,64,1024]{2,1,0:T(8,128)(2,1)}, bf16[1,64,1024]{2,1,0:T(8,128)(2,1)}, u32[]{:S(2)}, u32[]{:S(2)}) collective-permute-start(bf16[1,64,1024]{2,1,0:T(8,128)(2,1)} %get-tuple-element.57), channel_id=1, source_target_pairs={{0,16},{2,18},{4,20},{6,22},{8,24},{10,26},{12,28},{14,30},{16,0},... | collective-permute-start | bytes 393224 | tf_op jit(solution)/shard_map/ppermute | solution.py:333
  338.3 14.9 %collective-permute-start.29 = (bf16[1,64,1024]{2,1,0:T(8,128)(2,1)}, bf16[1,64,1024]{2,1,0:T(8,128)(2,1)}, u32[]{:S(2)}, u32[]{:S(2)}) collective-permute-start(bf16[1,64,1024]{2,1,0:T(8,128)(2,1)} %get-tuple-element.56), channel_id=1, source_target_pairs={{0,24},{2,26},{4,28},{6,30},{8,0},{10,2},{12,4},{14,6},{16,8},{18,... | collective-permute-start | bytes 393224 | tf_op jit(solution)/shard_map/ppermute | solution.py:333
  340.6 15.5 %collective-permute-start.32 = (bf16[1,64,1024]{2,1,0:T(8,128)(2,1)}, bf16[1,64,1024]{2,1,0:T(8,128)(2,1)}, u32[]{:S(2)}, u32[]{:S(2)}) collective-permute-start(bf16[1,64,1024]{2,1,0:T(8,128)(2,1)} %get-tuple-element.58), channel_id=1, source_target_pairs={{0,8},{2,10},{4,12},{6,14},{8,16},{10,18},{12,20},{14,22},{16,24},... | collective-permute-start | bytes 393224 | tf_op jit(solution)/shard_map/ppermute | solution.py:333
  347.3 26.4 %collective-permute-start.16 = (bf16[8,128,512]{2,1,0:T(8,128)(2,1)}, bf16[8,128,512]{2,1,0:T(8,128)(2,1)}, u32[]{:S(2)}, u32[]{:S(2)}) collective-permute-start(bf16[8,128,512]{2,1,0:T(8,128)(2,1)} %get-tuple-element.35), channel_id=1, source_target_pairs={{0,1},{1,0},{2,3},{3,2},{4,5},{5,4},{6,7},{7,6},{8,9},{9,8},{10,11... | collective-permute-start | bytes 3145736 | tf_op jit(solution)/shard_map/ppermute | solution.py:435
  349.0 47.2 %collective-permute-start.15 = (bf16[8,128,512]{2,1,0:T(8,128)(2,1)}, bf16[8,128,512]{2,1,0:T(8,128)(2,1)}, u32[]{:S(2)}, u32[]{:S(2)}) collective-permute-start(bf16[8,128,512]{2,1,0:T(8,128)(2,1)} %get-tuple-element.34), channel_id=1, source_target_pairs={{0,1},{1,0},{2,3},{3,2},{4,5},{5,4},{6,7},{7,6},{8,9},{9,8},{10,11... | collective-permute-start | bytes 3145736 | tf_op jit(solution)/shard_map/ppermute | solution.py:435
  351.5 67.1 %collective-permute-start.18 = (bf16[8,128,512]{2,1,0:T(8,128)(2,1)}, bf16[8,128,512]{2,1,0:T(8,128)(2,1)}, u32[]{:S(2)}, u32[]{:S(2)}) collective-permute-start(bf16[8,128,512]{2,1,0:T(8,128)(2,1)} %get-tuple-element.37), channel_id=1, source_target_pairs={{0,1},{1,0},{2,3},{3,2},{4,5},{5,4},{6,7},{7,6},{8,9},{9,8},{10,11... | collective-permute-start | bytes 3145736 | tf_op jit(solution)/shard_map/ppermute | solution.py:435
  353.1 82.5 %collective-permute-start.17 = (bf16[8,128,512]{2,1,0:T(8,128)(2,1)}, bf16[8,128,512]{2,1,0:T(8,128)(2,1)}, u32[]{:S(2)}, u32[]{:S(2)}) collective-permute-start(bf16[8,128,512]{2,1,0:T(8,128)(2,1)} %get-tuple-element.36), channel_id=1, source_target_pairs={{0,1},{1,0},{2,3},{3,2},{4,5},{5,4},{6,7},{7,6},{8,9},{9,8},{10,11... | collective-permute-start | bytes 3145736 | tf_op jit(solution)/shard_map/ppermute | solution.py:435
  356.1 6.9 %collective-permute-start.33 = (bf16[1,64,1024]{2,1,0:T(8,128)(2,1)}, bf16[1,64,1024]{2,1,0:T(8,128)(2,1)S(1)}, u32[]{:S(2)}, u32[]{:S(2)}) collective-permute-start(bf16[1,64,1024]{2,1,0:T(8,128)(2,1)} %get-tuple-element.60), channel_id=1, source_target_pairs={{0,16},{2,18},{4,20},{6,22},{8,24},{10,26},{12,28},{14,30},{16,0},... | collective-permute-start | bytes 393224 | tf_op jit(solution)/shard_map/ppermute | solution.py:333
  362.9 9.0 %collective-permute-start.34 = (bf16[1,64,1024]{2,1,0:T(8,128)(2,1)S(1)}, bf16[1,64,1024]{2,1,0:T(8,128)(2,1)S(1)}, u32[]{:S(2)}, u32[]{:S(2)}) collective-permute-start(bf16[1,64,1024]{2,1,0:T(8,128)(2,1)S(1)} %copy-done.20), channel_id=1, source_target_pairs={{0,24},{2,26},{4,28},{6,30},{8,0},{10,2},{12,4},{14,6},{16,8},{18,... | collective-permute-start | bytes 393224 | tf_op jit(solution)/shard_map/ppermute | solution.py:333
  371.9 75.8 %collective-permute-start.35 = (bf16[3,64,512]{2,1,0:T(8,128)(2,1)S(1)}, bf16[3,64,512]{2,1,0:T(8,128)(2,1)S(1)}, u32[]{:S(2)}, u32[]{:S(2)}) collective-permute-start(bf16[3,64,512]{2,1,0:T(8,128)(2,1)S(1)} %get-tuple-element.72), channel_id=1, source_target_pairs={{0,1},{1,0},{2,3},{3,2},{4,5},{5,4},{6,7},{7,6},{8,9},{9,8},{10,11... | collective-permute-start | bytes 589832 | tf_op jit(solution)/shard_map/ppermute | solution.py:448
  373.7 74.0 %collective-permute-start.36 = (bf16[1,64,512]{2,1,0:T(8,128)(2,1)S(1)}, bf16[1,64,512]{2,1,0:T(8,128)(2,1)S(1)}, u32[]{:S(2)}, u32[]{:S(2)}) collective-permute-start(bf16[1,64,512]{2,1,0:T(8,128)(2,1)S(1)} %get-tuple-element.74), channel_id=1, source_target_pairs={{0,1},{1,0},{2,3},{3,2},{4,5},{5,4},{6,7},{7,6},{8,9},{9,8},{10,11... | collective-permute-start | bytes 196616 | tf_op jit(solution)/shard_map/ppermute | solution.py:448
  (16 other events, 311.8 us)
